TPU v7x, 32 devices: a whole 2x2x4 slice. The times are simulated.
32 devices in a mesh: dp: 4 (over y, core), seq: 8 (over z, x).
Axes of the slice: x: 2, y: 2, z: 4, core: 2. Of those that a mesh axis runs over, the one named last changes fastest.
Arguments:
- tokens: bfloat16 [8, 1024, 1152], P('dp', 'seq'), may hold values from -6 to 6
- teacher: bfloat16 [8, 1024, 1152], P('dp', 'seq'), may hold values from -6 to 6
- lengths: int32 [8], P('dp'), may hold values from 256 to 1024, as said below
- w_query: bfloat16 [1152, 1152], P('dp', 'seq'), may hold values from -0.1875 to 0.1875
- key_weight: bfloat16 [1152, 384], P('dp', 'seq'), may hold values from -0.1875 to 0.1875
- value_weight: bfloat16 [1152, 384], P('dp', 'seq'), may hold values from -0.1875 to 0.1875
- w_out: bfloat16 [1152, 1152], P('dp', 'seq'), may hold values from -0.5 to 0.5
- w_gate: bfloat16 [1152, 3072], P('dp', 'seq'), may hold values from -0.1875 to 0.1875
- w_up: bfloat16 [1152, 3072], P('dp', 'seq'), may hold values from -0.1875 to 0.1875
- w_down: bfloat16 [3072, 1152], P('dp', 'seq'), may hold values from -0.109375 to 0.109375
- gain_attn: bfloat16 [1152], P('seq'), may hold values from 0.5 to 1.5
- gain_ffn: bfloat16 [1152], P('seq'), may hold values from 0.5 to 1.5
Outputs:
- output: bfloat16 [8, 1024, 1152], P('dp', 'seq')
- loss: float32 [], replicated
- tokens_grad: float32 [8, 1024, 1152], P('dp', 'seq')
- grad_w_query: float32 [1152, 1152], P('dp', 'seq')
- grad_w_key: float32 [1152, 384], P('dp', 'seq')
- grad_w_value: float32 [1152, 384], P('dp', 'seq')
- grad_w_out: float32 [1152, 1152], P('dp', 'seq')
- grad_w_gate: float32 [1152, 3072], P('dp', 'seq')
- grad_w_up: float32 [1152, 3072], P('dp', 'seq')
- grad_w_down: float32 [3072, 1152], P('dp', 'seq')
- grad_gain_attn: float32 [1152], P('seq')
- grad_gain_ffn: float32 [1152], P('seq')
Inputs may be any that keep to these rules, and one draw needn't show every extreme that they name: Slot s holds valid tokens at positions below lengths[s]; some slot has exactly 1024 and some exactly 256.
All inputs are finite; a program needn't handle non-finite values.
Results may differ from a plain program's by a relative error of at most 0.015.
Values may be sent and summed in bfloat16 or wider, within the bound.
A program may use at most 192 MiB of HBM per device.

v0:
```python
import math

import jax
import jax.numpy as jnp
from jax import lax
from jax.experimental import pallas as pl
from jax.experimental.pallas import tpu as pltpu
from jax.sharding import PartitionSpec as P

QUERY_HEADS = 18
KEY_VALUE_HEADS = 6
HEAD_DIMENSION = 64


norm_eps = 1e-05
rope_base = 10000.0


def rope_tables(positions, head_width):
    half_width = head_width // 2
    exponents = jnp.arange(half_width, dtype=jnp.float32) * (2.0 / head_width)
    angles = positions.astype(jnp.float32)[:, None] * (rope_base ** (-exponents))[None, :]
    return (jnp.cos(angles), jnp.sin(angles))


def apply_rotary(value_rows, cosine_table, sine_table):
    half_width = value_rows.shape[-1] // 2
    front_half = value_rows[..., :half_width]
    back_half = value_rows[..., half_width:]
    cos_wide = cosine_table[:, None, :]
    sin_wide = sine_table[:, None, :]
    return jnp.concatenate(
        [
            front_half * cos_wide - back_half * sin_wide,
            front_half * sin_wide + back_half * cos_wide,
        ],
        axis=-1,
    )


def allowed_mask(query_pos, key_pos, live_len):
    causal = key_pos[None, :] <= query_pos[:, None]
    present = key_pos[None, :] < live_len[:, None]
    return (causal[None, :, :] & present[:, None, :])[:, None, None, :, :]


def over_blocks(piece_len, unit_len, step_fn, running):
    block_length = math.gcd(piece_len, unit_len * max(1, 512 // unit_len))
    number_of_blocks = piece_len // block_length

    def loop_step(block_number, state):
        return step_fn(state, block_number * block_length, block_length)

    return lax.fori_loop(0, number_of_blocks, loop_step, running)


def collect(shards):
    wide = (
        lax.all_gather(shards[0], "seq", axis=1, tiled=True),
        lax.all_gather(shards[1], "seq", axis=1, tiled=True),
        lax.all_gather(shards[2], "seq", axis=1, tiled=True),
        lax.all_gather(shards[3], "seq", axis=1, tiled=True),
        lax.all_gather(shards[4], "seq", axis=1, tiled=True),
        lax.all_gather(shards[5], "seq", axis=1, tiled=True),
        lax.all_gather(shards[6], "seq", axis=1, tiled=True),
        lax.all_gather(shards[7], "seq", axis=0, tiled=True),
        lax.all_gather(shards[8], "seq", axis=0, tiled=True),
    )
    whole = (
        lax.all_gather(wide[0], "dp", axis=0, tiled=True),
        lax.all_gather(wide[1], "dp", axis=0, tiled=True),
        lax.all_gather(wide[2], "dp", axis=0, tiled=True),
        lax.all_gather(wide[3], "dp", axis=0, tiled=True),
        lax.all_gather(wide[4], "dp", axis=0, tiled=True),
        lax.all_gather(wide[5], "dp", axis=0, tiled=True),
        lax.all_gather(wide[6], "dp", axis=0, tiled=True),
    )
    return tuple(whole) + (wide[7], wide[8])


def reduce_grads(grad_sums):
    summed = (
        lax.psum_scatter(grad_sums[0], "seq", scatter_dimension=1, tiled=True),
        lax.psum_scatter(grad_sums[1], "seq", scatter_dimension=1, tiled=True),
        lax.psum_scatter(grad_sums[2], "seq", scatter_dimension=1, tiled=True),
        lax.psum_scatter(grad_sums[3], "seq", scatter_dimension=1, tiled=True),
        lax.psum_scatter(grad_sums[4], "seq", scatter_dimension=1, tiled=True),
        lax.psum_scatter(grad_sums[5], "seq", scatter_dimension=1, tiled=True),
        lax.psum_scatter(grad_sums[6], "seq", scatter_dimension=1, tiled=True),
        lax.psum_scatter(grad_sums[7], "seq", scatter_dimension=0, tiled=True),
        lax.psum_scatter(grad_sums[8], "seq", scatter_dimension=0, tiled=True),
    )
    owned = (
        lax.psum_scatter(summed[0], "dp", scatter_dimension=0, tiled=True),
        lax.psum_scatter(summed[1], "dp", scatter_dimension=0, tiled=True),
        lax.psum_scatter(summed[2], "dp", scatter_dimension=0, tiled=True),
        lax.psum_scatter(summed[3], "dp", scatter_dimension=0, tiled=True),
        lax.psum_scatter(summed[4], "dp", scatter_dimension=0, tiled=True),
        lax.psum_scatter(summed[5], "dp", scatter_dimension=0, tiled=True),
        lax.psum_scatter(summed[6], "dp", scatter_dimension=0, tiled=True),
    )
    return (tuple(owned), summed[7], summed[8])


def forward_slot(weights, tok_part, live_len, query_pos, cosine_table, sine_table):
    (
        full_query,
        full_key,
        full_value,
        full_out,
        full_gate,
        full_up,
        full_down,
        full_gain_attn,
        full_gain_ffn,
    ) = weights
    slot_position, stretched_length, model_width = tok_part.shape
    number_of_rows = slot_position * stretched_length
    query_group = QUERY_HEADS // KEY_VALUE_HEADS
    scale = HEAD_DIMENSION ** (-0.5)
    tok_float = tok_part.astype(jnp.float32).reshape(number_of_rows, model_width)
    inv_first = lax.rsqrt(jnp.mean(tok_float * tok_float, axis=-1, keepdims=True) + norm_eps)
    normed_first = tok_float * inv_first
    attention_input = (normed_first * full_gain_attn.astype(jnp.float32)).astype(jnp.bfloat16)
    unrotated_query = jnp.dot(
        attention_input, full_query, preferred_element_type=jnp.float32
    ).reshape(slot_position, stretched_length, QUERY_HEADS, HEAD_DIMENSION)
    unrotated_key = jnp.dot(attention_input, full_key, preferred_element_type=jnp.float32).reshape(
        slot_position, stretched_length, KEY_VALUE_HEADS, HEAD_DIMENSION
    )
    value_block = (
        jnp.dot(attention_input, full_value, preferred_element_type=jnp.float32)
        .astype(jnp.bfloat16)
        .reshape(slot_position, stretched_length, KEY_VALUE_HEADS * HEAD_DIMENSION)
    )
    query_b = (
        apply_rotary(unrotated_query, cosine_table, sine_table)
        .astype(jnp.bfloat16)
        .reshape(slot_position, stretched_length, KEY_VALUE_HEADS, query_group, HEAD_DIMENSION)
    )
    key_block = (
        apply_rotary(unrotated_key, cosine_table, sine_table)
        .astype(jnp.bfloat16)
        .reshape(slot_position, stretched_length, KEY_VALUE_HEADS * HEAD_DIMENSION)
    )
    empty_denominator = jnp.zeros(
        (slot_position, KEY_VALUE_HEADS, query_group, stretched_length), jnp.float32
    )
    empty_numerator = jnp.zeros(
        (slot_position, KEY_VALUE_HEADS, query_group, stretched_length, HEAD_DIMENSION), jnp.float32
    )
    key_piece = lax.all_gather(key_block, "seq", axis=1, tiled=True)
    value_piece = lax.all_gather(value_block, "seq", axis=1, tiled=True)

    def one_block(partial_value, offset, block_length):
        denominator, numerator = partial_value
        key_blk = lax.dynamic_slice_in_dim(key_piece, offset, block_length, 1).reshape(
            slot_position, block_length, KEY_VALUE_HEADS, HEAD_DIMENSION
        )
        value_blk = lax.dynamic_slice_in_dim(value_piece, offset, block_length, 1).reshape(
            slot_position, block_length, KEY_VALUE_HEADS, HEAD_DIMENSION
        )
        allowed = allowed_mask(
            query_pos, offset + jnp.arange(block_length, dtype=jnp.int32), live_len
        )
        scores = (
            jnp.einsum("schgd,snhd->shgcn", query_b, key_blk, preferred_element_type=jnp.float32)
            * scale
        )
        exp_scores = jnp.where(allowed, jnp.exp(scores), 0.0)
        denominator = denominator + jnp.sum(exp_scores, axis=-1)
        numerator = numerator + jnp.einsum(
            "shgcn,snhd->shgcd",
            exp_scores.astype(jnp.bfloat16),
            value_blk,
            preferred_element_type=jnp.float32,
        )
        return (denominator, numerator)

    denominator, numerator = over_blocks(
        key_piece.shape[1], stretched_length, one_block, (empty_denominator, empty_numerator)
    )
    attn_float = jnp.transpose(numerator / denominator[..., None], (0, 3, 1, 2, 4)).reshape(
        number_of_rows, QUERY_HEADS * HEAD_DIMENSION
    )
    attn_b = attn_float.astype(jnp.bfloat16)
    hidden = tok_float + jnp.dot(attn_b, full_out, preferred_element_type=jnp.float32)
    inv_second = lax.rsqrt(jnp.mean(hidden * hidden, axis=-1, keepdims=True) + norm_eps)
    normed_second = hidden * inv_second
    ffn_in = (normed_second * full_gain_ffn.astype(jnp.float32)).astype(jnp.bfloat16)
    gate_proj = jnp.dot(ffn_in, full_gate, preferred_element_type=jnp.float32)
    up_proj = jnp.dot(ffn_in, full_up, preferred_element_type=jnp.float32)
    hid_b = (jax.nn.silu(gate_proj) * up_proj).astype(jnp.bfloat16)
    valid_rows = (query_pos[None, :] < live_len[:, None]).reshape(number_of_rows, 1)
    out_float = jnp.where(
        valid_rows, hidden + jnp.dot(hid_b, full_down, preferred_element_type=jnp.float32), 0.0
    )
    saved = (
        attention_input,
        inv_first,
        normed_first,
        query_b,
        key_block,
        value_block,
        attn_float,
        attn_b,
        denominator,
        normed_second,
        inv_second,
        ffn_in,
        gate_proj,
        up_proj,
        hid_b,
    )
    return (out_float, valid_rows, saved)


def backward_slot(weights, saved, cotangent, live_len, query_pos, cosine_table, sine_table):
    (
        full_query,
        full_key,
        full_value,
        full_out,
        full_gate,
        full_up,
        full_down,
        full_gain_attn,
        full_gain_ffn,
    ) = weights
    (
        attention_input,
        inv_first,
        normed_first,
        query_b,
        key_block,
        value_block,
        attn_float,
        attn_b,
        denominator,
        normed_second,
        inv_second,
        ffn_in,
        gate_proj,
        up_proj,
        hid_b,
    ) = saved
    slot_position = query_b.shape[0]
    stretched_length = query_b.shape[1]
    number_of_rows = slot_position * stretched_length
    query_group = QUERY_HEADS // KEY_VALUE_HEADS
    scale = HEAD_DIMENSION ** (-0.5)
    cot_b = cotangent.astype(jnp.bfloat16)
    grad_down = jnp.einsum("rf,rd->fd", hid_b, cot_b, preferred_element_type=jnp.float32)
    grad_hid = jnp.einsum("rd,fd->rf", cot_b, full_down, preferred_element_type=jnp.float32)
    sigmoid_gate = jax.nn.sigmoid(gate_proj)
    grad_gate_b = (
        grad_hid * up_proj * sigmoid_gate * (1.0 + gate_proj * (1.0 - sigmoid_gate))
    ).astype(jnp.bfloat16)
    grad_up_b = (grad_hid * gate_proj * sigmoid_gate).astype(jnp.bfloat16)
    grad_gate = jnp.einsum("rd,rf->df", ffn_in, grad_gate_b, preferred_element_type=jnp.float32)
    grad_up = jnp.einsum("rd,rf->df", ffn_in, grad_up_b, preferred_element_type=jnp.float32)
    grad_ffn_in = jnp.einsum(
        "rf,df->rd", grad_gate_b, full_gate, preferred_element_type=jnp.float32
    ) + jnp.einsum("rf,df->rd", grad_up_b, full_up, preferred_element_type=jnp.float32)
    grad_gain_ffn = jnp.sum(grad_ffn_in * normed_second, axis=0)
    grad_normed = grad_ffn_in * full_gain_ffn.astype(jnp.float32)
    grad_hidden = cotangent + inv_second * (
        grad_normed - normed_second * jnp.mean(grad_normed * normed_second, axis=-1, keepdims=True)
    )
    grad_proj_b = grad_hidden.astype(jnp.bfloat16)
    grad_out = jnp.einsum("rq,rd->qd", attn_b, grad_proj_b, preferred_element_type=jnp.float32)
    grad_attn_b = jnp.einsum(
        "rd,qd->rq", grad_proj_b, full_out, preferred_element_type=jnp.float32
    ).astype(jnp.bfloat16)
    den_rows = jnp.transpose(denominator, (0, 3, 1, 2)).reshape(number_of_rows, QUERY_HEADS)
    grad_heads_float = grad_attn_b.astype(jnp.float32).reshape(
        number_of_rows, QUERY_HEADS, HEAD_DIMENSION
    )
    softmax_ratio = (
        jnp.sum(
            grad_heads_float * attn_float.reshape(number_of_rows, QUERY_HEADS, HEAD_DIMENSION),
            axis=-1,
        )
        / den_rows
    ).reshape(slot_position, stretched_length, QUERY_HEADS)
    scaled_gradient = (
        (grad_heads_float / den_rows[..., None])
        .astype(jnp.bfloat16)
        .reshape(slot_position, stretched_length, QUERY_HEADS * HEAD_DIMENSION)
    )
    ratio_all = lax.all_gather(softmax_ratio, "seq", axis=1, tiled=True)
    head_gradient = scaled_gradient.reshape(
        slot_position, stretched_length, KEY_VALUE_HEADS, query_group, HEAD_DIMENSION
    )
    local_softmax_ratio = jnp.transpose(
        softmax_ratio.reshape(slot_position, stretched_length, KEY_VALUE_HEADS, query_group),
        (0, 2, 3, 1),
    )[..., None]
    empty_query = jnp.zeros(
        (slot_position, KEY_VALUE_HEADS, query_group, stretched_length, HEAD_DIMENSION), jnp.float32
    )
    key_piece = lax.all_gather(key_block, "seq", axis=1, tiled=True)
    value_piece = lax.all_gather(value_block, "seq", axis=1, tiled=True)

    def one_block(partial_value, offset, block_length):
        key_blk = lax.dynamic_slice_in_dim(key_piece, offset, block_length, 1).reshape(
            slot_position, block_length, KEY_VALUE_HEADS, HEAD_DIMENSION
        )
        value_blk = lax.dynamic_slice_in_dim(value_piece, offset, block_length, 1).reshape(
            slot_position, block_length, KEY_VALUE_HEADS, HEAD_DIMENSION
        )
        allowed = allowed_mask(
            query_pos, offset + jnp.arange(block_length, dtype=jnp.int32), live_len
        )
        scores = (
            jnp.einsum("schgd,snhd->shgcn", query_b, key_blk, preferred_element_type=jnp.float32)
            * scale
        )
        exp_scores = jnp.where(allowed, jnp.exp(scores), 0.0)
        grad_prob = jnp.einsum(
            "schgd,snhd->shgcn", head_gradient, value_blk, preferred_element_type=jnp.float32
        )
        grad_score = (exp_scores * (grad_prob - local_softmax_ratio)).astype(jnp.bfloat16)
        return (
            partial_value
            + jnp.einsum(
                "shgcn,snhd->shgcd", grad_score, key_blk, preferred_element_type=jnp.float32
            )
            * scale
        )

    grad_query = over_blocks(key_piece.shape[1], stretched_length, one_block, empty_query)
    query_flat = query_b.reshape(slot_position, stretched_length, QUERY_HEADS * HEAD_DIMENSION)
    per_head_keys = key_block.reshape(
        slot_position, stretched_length, KEY_VALUE_HEADS, HEAD_DIMENSION
    )
    per_head_values = value_block.reshape(
        slot_position, stretched_length, KEY_VALUE_HEADS, HEAD_DIMENSION
    )
    empty_key_value = jnp.zeros(
        (slot_position, KEY_VALUE_HEADS, stretched_length, HEAD_DIMENSION), jnp.float32
    )
    query_piece = lax.all_gather(query_flat, "seq", axis=1, tiled=True)
    grad_piece = lax.all_gather(scaled_gradient, "seq", axis=1, tiled=True)

    def one_block(partial_value, offset, block_length):
        grad_key, value_gradient = partial_value
        query_blk = lax.dynamic_slice_in_dim(query_piece, offset, block_length, 1).reshape(
            slot_position, block_length, KEY_VALUE_HEADS, query_group, HEAD_DIMENSION
        )
        grad_blk = lax.dynamic_slice_in_dim(grad_piece, offset, block_length, 1).reshape(
            slot_position, block_length, KEY_VALUE_HEADS, query_group, HEAD_DIMENSION
        )
        ratio_blk = lax.dynamic_slice_in_dim(ratio_all, offset, block_length, 1).reshape(
            slot_position, block_length, KEY_VALUE_HEADS, query_group
        )
        ratio_blk = jnp.transpose(ratio_blk, (0, 2, 3, 1))[..., None]
        remote_pos = offset + jnp.arange(block_length, dtype=jnp.int32)
        allowed = allowed_mask(remote_pos, query_pos, live_len)
        scores = (
            jnp.einsum(
                "snhgd,schd->shgnc", query_blk, per_head_keys, preferred_element_type=jnp.float32
            )
            * scale
        )
        exp_scores = jnp.where(allowed, jnp.exp(scores), 0.0)
        value_gradient = value_gradient + jnp.einsum(
            "shgnc,snhgd->shcd",
            exp_scores.astype(jnp.bfloat16),
            grad_blk,
            preferred_element_type=jnp.float32,
        )
        grad_prob = jnp.einsum(
            "snhgd,schd->shgnc", grad_blk, per_head_values, preferred_element_type=jnp.float32
        )
        grad_score = (exp_scores * (grad_prob - ratio_blk)).astype(jnp.bfloat16)
        grad_key = (
            grad_key
            + jnp.einsum(
                "shgnc,snhgd->shcd", grad_score, query_blk, preferred_element_type=jnp.float32
            )
            * scale
        )
        return (grad_key, value_gradient)

    grad_key, value_gradient = over_blocks(
        query_piece.shape[1], stretched_length, one_block, (empty_key_value, empty_key_value)
    )
    grad_query = jnp.transpose(grad_query, (0, 3, 1, 2, 4)).reshape(
        slot_position, stretched_length, QUERY_HEADS, HEAD_DIMENSION
    )
    grad_query_b = (
        apply_rotary(grad_query, cosine_table, -sine_table)
        .astype(jnp.bfloat16)
        .reshape(number_of_rows, QUERY_HEADS * HEAD_DIMENSION)
    )
    grad_key_b = (
        apply_rotary(jnp.transpose(grad_key, (0, 2, 1, 3)), cosine_table, -sine_table)
        .astype(jnp.bfloat16)
        .reshape(number_of_rows, KEY_VALUE_HEADS * HEAD_DIMENSION)
    )
    grad_value_b = (
        jnp.transpose(value_gradient, (0, 2, 1, 3))
        .astype(jnp.bfloat16)
        .reshape(number_of_rows, KEY_VALUE_HEADS * HEAD_DIMENSION)
    )
    grad_wq = jnp.einsum(
        "rd,rq->dq", attention_input, grad_query_b, preferred_element_type=jnp.float32
    )
    grad_wk = jnp.einsum(
        "rd,rq->dq", attention_input, grad_key_b, preferred_element_type=jnp.float32
    )
    grad_wv = jnp.einsum(
        "rd,rq->dq", attention_input, grad_value_b, preferred_element_type=jnp.float32
    )
    grad_attn_in = jnp.einsum(
        "rq,dq->rd", grad_query_b, full_query, preferred_element_type=jnp.float32
    )
    grad_attn_in = grad_attn_in + jnp.einsum(
        "rq,dq->rd", grad_key_b, full_key, preferred_element_type=jnp.float32
    )
    grad_attn_in = grad_attn_in + jnp.einsum(
        "rq,dq->rd", grad_value_b, full_value, preferred_element_type=jnp.float32
    )
    grad_gain_attn = jnp.sum(grad_attn_in * normed_first, axis=0)
    grad_first = grad_attn_in * full_gain_attn.astype(jnp.float32)
    grad_tokens = grad_hidden + inv_first * (
        grad_first - normed_first * jnp.mean(grad_first * normed_first, axis=-1, keepdims=True)
    )
    return (
        (
            grad_wq,
            grad_wk,
            grad_wv,
            grad_out,
            grad_gate,
            grad_up,
            grad_down,
            grad_gain_attn,
            grad_gain_ffn,
        ),
        grad_tokens,
    )


def per_device(
    tokens,
    teacher,
    lengths,
    w_query,
    key_weight,
    value_weight,
    w_out,
    w_gate,
    w_up,
    w_down,
    gain_attn,
    gain_ffn,
):
    shards = (w_query, key_weight, value_weight, w_out, w_gate, w_up, w_down, gain_attn, gain_ffn)
    slot_count, stretched_length, model_width = tokens.shape
    total_tokens = slot_count * lax.axis_size("dp") * stretched_length * lax.axis_size("seq")
    query_pos = lax.axis_index("seq") * stretched_length + jnp.arange(
        stretched_length, dtype=jnp.int32
    )
    cosine_table, sine_table = rope_tables(query_pos, HEAD_DIMENSION)
    out_rows = []
    stored = []
    differences = []
    squares_local = jnp.zeros((), jnp.float32)
    count_local = jnp.zeros((), jnp.float32)
    for micro in range(slot_count):
        weights = collect(shards)
        live_len = lengths[micro : micro + 1]
        out_float, valid_rows, saved = forward_slot(
            weights, tokens[micro : micro + 1], live_len, query_pos, cosine_table, sine_table
        )
        teach_float = teacher[micro].astype(jnp.float32)
        difference = jnp.where(valid_rows, out_float - teach_float, 0.0)
        squares_local = squares_local + jnp.sum(difference * difference)
        count_local = count_local + jnp.sum(valid_rows.astype(jnp.float32))
        out_rows.append(out_float.astype(jnp.bfloat16).reshape(1, stretched_length, model_width))
        stored.append(saved)
        differences.append(difference)
    loss_sum, count_sum = lax.psum((squares_local, count_local), ("dp", "seq"))
    loss = loss_sum / count_sum
    factor = total_tokens / count_sum
    grad_sums = None
    token_grads = []
    for micro in range(slot_count):
        weights = collect(shards)
        grads, grad_tokens = backward_slot(
            weights,
            stored[micro],
            factor * differences[micro],
            lengths[micro : micro + 1],
            query_pos,
            cosine_table,
            sine_table,
        )
        grad_sums = grads if grad_sums is None else jax.tree.map(jnp.add, grad_sums, grads)
        token_grads.append(grad_tokens.reshape(1, stretched_length, model_width))
    owned, gain_part_attn, gain_part_ffn = reduce_grads(grad_sums)
    gain_totals = lax.psum((gain_part_attn, gain_part_ffn), "dp")
    output = jnp.concatenate(out_rows, axis=0)
    tokens_grad = jnp.concatenate(token_grads, axis=0)
    return (
        output,
        loss,
        tokens_grad,
        owned[0],
        owned[1],
        owned[2],
        owned[3],
        owned[4],
        owned[5],
        owned[6],
        gain_totals[0],
        gain_totals[1],
    )


MESH_ID = pl.DeviceIdType.MESH
VMEM_MOST = 64 * 1024 * 1024 - 128 * 1024


class Place(tuple):
    def with_line(self):
        z = self[2]
        self.line = (0,) + tuple(pick(z, v) for v in ((1, -1, -1, -1), (2, 1, 1, -2), (3, 2, -2, -3)))
        self.sign = (0,) + tuple(jnp.where(offset > 0, 1, -1) for offset in self.line[1:])
        return self


def position():
    row = lax.axis_index("dp")
    column = lax.axis_index("seq")
    return Place((lax.rem(column, 2), row // 2, column // 2, lax.rem(row, 2))).with_line()


def mesh_place(x, y, z, c):
    return (2 * y + c, 2 * z + x)


def step_to(place, axis, sign=1):
    x, y, z, c = place
    if axis == "x":
        return (1 - x, y, z, c)
    if axis == "y":
        return (x, 1 - y, z, c)
    if axis == "z":
        return (x, y, z + sign, c)
    return (x, y, z, 1 - c)


def pick(z, values):
    return sum(jnp.where(z == i, v, 0) for i, v in enumerate(values) if v)


def shifted(place, rel):
    x, y, z, c = place
    dx, dy, rank = rel
    return ((1 - x) if dx else x, (1 - y) if dy else y, z + place.line[rank], c)


def on_line(z):
    return jnp.logical_and(z >= 0, z < 4)


def greet(place, lines):
    x, y, z, c = place
    d, s = mesh_place(*place)
    barrier = pltpu.get_barrier_semaphore()

    def signal(who):
        pl.semaphore_signal(barrier, inc=1, device_id=who, device_id_type=MESH_ID)

    if lines:
        for k in range(1, 8):
            signal((d, lax.rem(s + k, 8)))
        for k in range(1, 4):
            signal((lax.rem(d + k, 4), s))
        pl.semaphore_wait(barrier, 10)
        return
    for axis in "xyc":
        signal(mesh_place(*step_to(place, axis)))
    pl.when(z < 3)(lambda: signal(mesh_place(x, y, z + 1, c)))
    pl.when(z > 0)(lambda: signal(mesh_place(x, y, z - 1, c)))
    pl.semaphore_wait(barrier, 3 + jnp.where(z > 0, 1, 0) + jnp.where(z < 3, 1, 0))


def wait_bytes(region, sem):
    pltpu.make_async_copy(region, region, sem).wait()


def spread_order(order):
    held = [((0, 0, 0), -1)]
    for level, axis in enumerate(order):
        new = []
        if axis == "z":
            new = [((rel[0], rel[1], rank), level) for rank in (1, 2, 3) for rel, _ in held]
        else:
            new = [((1, rel[1], rel[2]) if axis == "x" else (rel[0], 1, rel[2]), level) for rel, _ in held]
        held = held + new
    return held


class Spread:
    def __init__(self, place, order, own, spot, sems, job, pair=None, amount=None):
        self.place, self.order, self.own, self.spot = place, order, own, spot
        self.recv, self.send, self.recv_core, self.send_core = sems
        self.job, self.pair, self.amount = job, pair, amount
        self.pieces = spread_order(order)

    def number(self, who):
        x, y, z, _ = who
        return z * 4 + y * 2 + x

    def go(self, rel, level, target):
        who = shifted(self.place, rel)
        pltpu.make_async_remote_copy(
            src_ref=self.own if level < 0 else self.spot(who),
            dst_ref=self.spot(who),
            send_sem=self.send.at[self.job],
            recv_sem=self.recv.at[self.job, self.number(who)],
            device_id=mesh_place(*target),
            device_id_type=MESH_ID,
        ).start()

    def to_core(self, rel):
        who = shifted(self.place, rel)
        pltpu.make_async_remote_copy(
            src_ref=self.pair(who),
            dst_ref=self.pair(who),
            send_sem=self.send_core.at[self.job],
            recv_sem=self.recv_core.at[self.job],
            device_id=mesh_place(*step_to(self.place, "c")),
            device_id_type=MESH_ID,
        ).start()

    def steps(self):
        out = []
        arrived = set()
        z = self.place[2]
        for rel, level in self.pieces:

            def run(rel=rel, level=level):
                arrived.add(rel)
                who = shifted(self.place, rel)
                if level >= 0:
                    there = self.spot(who)
                    pltpu.make_async_copy(there, there, self.recv.at[self.job, self.number(who)]).wait()
                if level >= 0 and self.order[level] == "z":
                    on = z - self.place.sign[rel[2]]
                    pl.when(on_line(on))(lambda: self.go(rel, level, (self.place[0], self.place[1], on, self.place[3])))
                for axis in self.order[level + 1:]:
                    if axis == "z":
                        pl.when(z < 3)(lambda: self.go(rel, level, step_to(self.place, "z", 1)))
                        pl.when(z > 0)(lambda: self.go(rel, level, step_to(self.place, "z", -1)))
                    else:
                        self.go(rel, level, step_to(self.place, axis))
                if self.pair is not None and (1 - rel[0], rel[1], rel[2]) in arrived:
                    self.to_core(rel)

            out.append(run)
        return out

    def sent(self):
        total = [0, 0]
        for i, z in enumerate((0, 1)):
            for rel, level in self.pieces:
                if level >= 0 and self.order[level] == "z":
                    offset = (0, ((1, -1)[z]), ((2, 1)[z]), ((3, 2)[z]))[rel[2]]
                    on = z - (1 if offset > 0 else -1)
                    total[i] += 0 <= on < 4
                for axis in self.order[level + 1:]:
                    total[i] += (1, 2)[z] if axis == "z" else 1
        return total

    def wait_core(self):
        wait_bytes(self.amount(16), self.recv_core.at[self.job])

    def finish(self):
        ends, inner = self.sent()
        z = self.place[2]
        at_end = jnp.logical_or(z == 0, z == 3)
        pl.when(at_end)(lambda: wait_bytes(self.amount(ends), self.send.at[self.job]))
        pl.when(jnp.logical_not(at_end))(lambda: wait_bytes(self.amount(inner), self.send.at[self.job]))
        if self.pair is not None:
            wait_bytes(self.amount(16), self.send_core.at[self.job])


def fold_pieces(order):
    out = []
    for dx in (0, 1):
        for dy in (0, 1) if "y" in order else (0,):
            for rank in (0, 1, 2, 3):
                differs = {"x": dx, "y": dy, "z": rank}
                stage = next((i for i, axis in enumerate(order) if differs[axis]), len(order))
                out.append(((dx, dy, rank), stage))
    return sorted(out, key=lambda item: (item[1], -item[0][2], -item[0][0] - item[0][1]))


def fold_slots(order):
    base, starts = 0, []
    for level, axis in enumerate(order):
        starts.append(base)
        after = order[level + 1:]
        wide = (4 if "z" in after else 1) * (2 if "x" in after else 1) * (2 if "y" in after else 1)
        base += wide * 5 if axis == "z" else wide
    return starts, base


class Fold:
    def __init__(self, place, order, mine, arrived, sems, job, out, amount, ready=None):
        self.place, self.order, self.mine, self.arrived = place, order, mine, arrived
        self.send, self.recv = sems
        self.job, self.out, self.amount, self.ready = job, out, amount, ready
        self.pieces = fold_pieces(order)
        self.base, self.slots = fold_slots(order)

    def slot(self, level, rel, last):
        index = 0
        at_z = self.place[2] + self.place.line[rel[2]]
        for other in self.order[level + 1:]:
            size = 4 if other == "z" else 2
            index = index * size + (at_z if other == "z" else (rel[0] if other == "x" else rel[1]))
        if self.order[level] == "z":
            index = index * 5 + (4 if last is True else (at_z if last is False else jnp.where(last, 4, at_z)))
        return self.base[level] + index

    def take(self, mine, slot):
        there = self.arrived.at[slot]
        pltpu.make_async_copy(there, there, self.recv.at[self.job, slot]).wait()
        mine[...] = mine[...] + self.arrived[slot]

    def steps(self):
        out = []
        present = set()
        z = self.place[2]
        for rel, stage in self.pieces:

            def run(rel=rel, stage=stage):
                if self.ready is not None and rel[1] not in present:
                    present.add(rel[1])
                    self.ready(rel[1])
                mine = self.mine(shifted(self.place, rel))
                offset, sign = self.place.line[rel[2]], self.place.sign[rel[2]]
                for level in range(min(stage + 1, len(self.order))):
                    if self.order[level] == "z":
                        if level < stage:
                            pl.when(z > 0)(lambda: self.take(mine, self.slot(level, rel, False)))
                            pl.when(z < 3)(lambda: self.take(mine, self.slot(level, rel, True)))
                        else:
                            behind = z - sign
                            pl.when(on_line(behind))(lambda: self.take(mine, self.slot(level, rel, False)))
                    elif level < stage:
                        self.take(mine, self.slot(level, rel, False))
                if stage == len(self.order):
                    self.out(mine[...].astype(jnp.float32))
                    return
                axis = self.order[stage]
                if axis == "z":
                    target = (self.place[0], self.place[1], z + sign, self.place[3])
                else:
                    target = step_to(self.place, axis)
                slot = self.slot(stage, rel, offset == -1 if axis == "z" else False)
                pltpu.make_async_remote_copy(
                    src_ref=mine,
                    dst_ref=self.arrived.at[slot],
                    send_sem=self.send.at[self.job],
                    recv_sem=self.recv.at[self.job, slot],
                    device_id=mesh_place(*target),
                    device_id_type=MESH_ID,
                ).start()

            out.append(run)
        return out

    def finish(self):
        wait_bytes(self.amount(len(self.pieces) - 1), self.send.at[self.job])


CAT_JOBS = (("cat", 0, 96, "xzy"), ("cat", 96, 96, "yzx"), ("cat", 192, 96, "zxy"))
FFN_JOBS = (
    ("gate", 0, 144, "xzy"), ("up", 0, 96, "yzx"), ("down", 0, 384, "zxy"),
    ("gate", 144, 144, "xzy"), ("up", 96, 96, "yzx"), ("down", 384, 384, "zxy"), ("up", 192, 96, "zxy"),
)
KV_JOBS = tuple((slot, 256 * third, "xz" if (slot, third) == (1, 2) else "zx") for slot in (0, 1) for third in (0, 1, 2))
FOLD_FFN = tuple(job[:3] + (job[3][::-1],) for job in FFN_JOBS)
FOLD_CAT = tuple(job[:3] + (job[3][::-1],) for job in CAT_JOBS)
FOLD_KV = tuple((slot, row, order[::-1]) for slot, row, order in KV_JOBS)
FFN_NAMES = ("gate", "up", "down")


def job_shape(job):
    return (144, job[2]) if job[0] == "down" else (job[2], 384)


def piece_of(ref, job, paired=False):
    name, first, count, _ = job
    double = 2 if paired else 1

    def spot(who):
        x, y, z, c = who
        d, s = mesh_place(0 if paired else x, y, z, c)
        if name == "down":
            return ref.at[
                pl.ds(pl.multiple_of(s * 144, 16), 144 * double), pl.ds(pl.multiple_of(d * 768 + first, 128), count)
            ]
        return ref.at[
            pl.ds(pl.multiple_of(d * 288 + first, 8), count), pl.ds(pl.multiple_of(s * 384, 128), 384 * double)
        ]

    return spot


def region(ref, elements, rows, columns):
    units = elements // 2048
    wide = max(k for k in range(1, columns // 128 + 1) if units % k == 0 and units // k <= rows // 16)
    return ref.at[pl.ds(0, units // wide * 16), pl.ds(0, wide * 128)]


def amount_of(ref, job):
    rows, columns = job_shape(job)
    return lambda pieces: region(ref, pieces * rows * columns, *ref.shape)


def own_part(ref, job):
    name, first, count, _ = job
    return ref.at[:, pl.ds(first, count)] if name == "down" else ref.at[pl.ds(first, count), :]


def kv_spot(ref, slot, row):
    def spot(who):
        _, s = mesh_place(*who)
        return ref.at[slot, pl.ds(row, 256), pl.ds(pl.multiple_of(s * 128, 128), 128)]

    return spot


def kv_amount(ref):
    return lambda pieces: ref.at[0, pl.ds(0, 32 * pieces), :]


def make_spreads(place, jobs, shards, wholes, sems):
    return [
        Spread(
            place, job[3], own_part(shards[job[0]], job), piece_of(wholes[job[0]], job), sems, j,
            piece_of(wholes[job[0]], job, True), amount_of(wholes[job[0]], job),
        )
        for j, job in enumerate(jobs)
    ]


def make_kv_spreads(place, own, whole, sems):
    return [
        Spread(
            place, order, own.at[pl.ds(row, 256), pl.ds(slot * 128, 128)], kv_spot(whole, slot, row),
            (sems[0], sems[1], None, None), j, None, kv_amount(whole),
        )
        for j, (slot, row, order) in enumerate(KV_JOBS)
    ]


def spread_sems(jobs):
    n = len(jobs)
    return [
        pltpu.SemaphoreType.DMA((n, 16)), pltpu.SemaphoreType.DMA((n,)),
        pltpu.SemaphoreType.DMA((n,)), pltpu.SemaphoreType.DMA((n,)),
    ]


def fold_scratch(jobs, paired):
    n = len(jobs)
    most = max(fold_slots(job[3])[1] for job in jobs)
    scratch = [
        pltpu.SemaphoreType.DMA((n,)), pltpu.SemaphoreType.DMA((n, most)),
        pltpu.SemaphoreType.DMA((n, 2)), pltpu.SemaphoreType.DMA((n, 2)), pltpu.SemaphoreType.DMA((n, 2)),
    ]
    for job in jobs:
        rows, columns = job_shape(job)
        block = (2, 1152, columns) if job[0] == "down" else (2, rows, 3072)
        scratch += [
            pltpu.VMEM(block, jnp.bfloat16), pltpu.VMEM((fold_slots(job[3])[1], rows, columns), jnp.bfloat16)
        ]
        scratch += [pltpu.VMEM(block, jnp.bfloat16)] if paired else []
    return scratch


class JobFold:
    def __init__(self, place, job, j, sums, owned, scratch, paired):
        self.place, self.job, self.j, self.sums, self.paired = place, job, j, sums, paired
        send, recv, self.load_sem, self.core_send, self.core_recv = scratch[:5]
        each = 3 if paired else 2
        self.acc, arrived = scratch[5 + each * j: 7 + each * j]
        self.other = scratch[7 + each * j] if paired else None
        name, first, count, order = job

        def mine(who):
            x, y, z, c = who
            s = 2 * z + x
            if name == "down":
                return self.acc.at[y, pl.ds(pl.multiple_of(s * 144, 16), 144), :]
            return self.acc.at[y, :, pl.ds(pl.multiple_of(s * 384, 128), 384)]

        def out(value):
            if name == "down":
                owned[:, first: first + count] = value
            else:
                owned[first: first + count, :] = value

        self.fold = Fold(place, order, mine, arrived, (send, recv), j, out, amount_of(sums, job), self.ready)

    def block(self, y, c):
        name, first, count, _ = self.job
        d = 2 * y + c if self.paired else y
        if name == "down":
            return self.sums.at[:, pl.ds(pl.multiple_of(d * 768 + first, 128), count)]
        return self.sums.at[pl.ds(pl.multiple_of(d * 288 + first, 8), count), :]

    def local_copy(self, dy):
        x, y, z, c = self.place
        at = (1 - y) if dy else y
        return pltpu.make_async_copy(self.block(at, c), self.acc.at[at], self.load_sem.at[self.j, dy])

    def core_copy(self, dy):
        x, y, z, c = self.place
        at = (1 - y) if dy else y
        return pltpu.make_async_remote_copy(
            src_ref=self.block(at, 1 - c),
            dst_ref=self.other.at[at],
            send_sem=self.core_send.at[self.j, dy],
            recv_sem=self.core_recv.at[self.j, dy],
            device_id=mesh_place(x, y, z, 1 - c),
            device_id_type=MESH_ID,
        )

    def begin(self, dy):
        if self.paired:
            self.core_copy(dy).start()
        self.local_copy(dy).start()

    def ready(self, dy):
        y = self.place[1]
        at = (1 - y) if dy else y
        self.local_copy(dy).wait()
        if not self.paired:
            return
        self.core_copy(dy).wait_recv()

        def add(k, _):
            if self.job[0] == "down":
                part = (at, pl.ds(pl.multiple_of(k * 144, 16), 144), slice(None))
            else:
                part = (at, slice(None), pl.ds(pl.multiple_of(k * 384, 128), 384))
            self.acc[part] = self.acc[part] + self.other[part]
            return _

        lax.fori_loop(0, 8, add, 0)

    def finish(self):
        self.fold.finish()
        for dy in (0, 1) if self.paired else ():
            self.core_copy(dy).wait_send()


class Notes:
    def __init__(self, place, tile_of, own, by_seq, by_dp, sems):
        self.d, self.s = mesh_place(*place)
        self.tile_of, self.own, self.by_seq, self.by_dp = tile_of, own, by_seq, by_dp
        self.seq_send, self.seq_recv, self.dp_send, self.dp_recv = sems

    def along_seq(self, k):
        peer = lax.rem(self.s + k, 8)
        return pltpu.make_async_remote_copy(
            src_ref=self.tile_of(peer), dst_ref=self.by_seq.at[self.s], send_sem=self.seq_send.at[k],
            recv_sem=self.seq_recv.at[self.s], device_id=(self.d, peer), device_id_type=MESH_ID,
        )

    def along_dp(self, k):
        peer = lax.rem(self.d + k, 4)
        return pltpu.make_async_remote_copy(
            src_ref=self.own, dst_ref=self.by_dp.at[self.d], send_sem=self.dp_send.at[k],
            recv_sem=self.dp_recv.at[self.d], device_id=(peer, self.s), device_id_type=MESH_ID,
        )

    def wait_seq(self):
        for k in range(1, 8):
            peer = lax.rem(self.s + k, 8)
            there = self.by_seq.at[peer]
            pltpu.make_async_copy(there, there, self.seq_recv.at[peer]).wait()

    def wait_dp(self):
        for k in range(1, 4):
            peer = lax.rem(self.d + k, 4)
            there = self.by_dp.at[peer]
            pltpu.make_async_copy(there, there, self.dp_recv.at[peer]).wait()


NOTE_SEMS = [
    pltpu.SemaphoreType.DMA((8,)), pltpu.SemaphoreType.DMA((8,)),
    pltpu.SemaphoreType.DMA((4,)), pltpu.SemaphoreType.DMA((4,)),
]


FORWARD_PLAN = (
    (0, 100, 200,),
    (108, 1, 2, 101, 102, 8, 201, 204, 208, 4, 3, 202, 9, 104, 103, 205, 10, 109, 110, 209, 5, 105, 206, 203,
        11, 210, 6, 212, 106, 112, 207, 7, 213, 107,),
    (10500, 113, 211, 114, 10000, 10600, 214, 115, 14, 111, 10100, 10200, 10300, 10400, 12, 215, 15, 13,),
    (20000, 20100, 20200, 20300, 20400, 20500,),
    (10002, 10001, 20001, 20101, 20002, 20004, 10504, 20201, 20104, 10204, 20301, 20204, 10102, 20401, 10501,
        20304, 10101, 10008, 10201, 20502, 10604, 20501, 20404, 10108, 10302, 10301, 10601, 10402, 10401,
        20102, 10508, 10004, 10208, 20202, 10308, 10408, 20302, 10608, 10104, 20402, 20005, 10202, 10009,
        20105, 10502, 20205, 10209, 10304, 10003, 10404, 10010, 10602, 20503, 20504, 20305, 20405, 10509,
        10103, 10309, 10505, 10205, 20003, 10609, 10303, 10109, 10110, 10310, 20103, 20006, 10605, 20203,
        10403, 20505, 20106, 10005, 20303, 10210, 20206, 10512, 10409, 10410, 10510, 10212, 20306, 10613,
        20406, 10506, 10203, 10105, 10503, 10612, 10206, 10305, 10610, 10012, 10405, 20403, 10603, 10606,
        20107, 10011, 10213, 20007, 10006, 10312, 20506, 20207, 10513, 10111, 10112, 20307, 10311, 10507,
        20507, 10511, 10411, 20407,),
    (
        (1, (10211, 10306, 10412,)),
        (2, (10207, 10106, 10013, 10607,)),
        (3, (10406,)),
        (5, (10007,)),
        (8, (10113,)),
        (9, (10107, 10514,)),
        (11, (10307, 10313,)),
    ),
    (10407, 10413, 10214, 10611, 10614, 10014, 10114, 10515, 10414, 10215, 10314, 10615, 10015, 10115, 10415, 10315,),
)
BACKWARD_PLAN = (
    (10100, 10101,),
    (
        (0, (10300,)),
        (3, (10000,)),
        (5, (10102, 10500,)),
        (8, (10200,)),
        (9, (10400,)),
    ),
    (10401, 20500, 10103, 10105, 10104, 20000, 10001, 10302, 20501, 20502, 10201, 10501, 10106, 10002, 20300,
        20100, 20200, 20400, 10202, 10502, 10600, 20504, 20503, 10003, 10304, 10306, 20001, 20101, 20201,
        20301, 20401, 10107, 10108, 10109, 10110, 20402, 20505, 10301, 10303, 10305, 20002, 20102, 20202,
        20302, 10203, 10503, 10004, 20506, 20303, 20304, 10204, 10402, 10504, 10005, 10111, 20003, 20103,
        20203, 20403, 20004, 20204, 20404, 20005, 20205, 10602, 10205, 10604, 20305, 10403, 10505, 10006,
        20405, 10307, 10308, 10601, 10603, 20006, 20104, 20105, 20106, 10112, 20206, 10206, 10309, 10404,
        20306, 10506, 10007, 10008, 20007, 20406, 10113, 10009, 10207, 10208, 10209, 10405, 10507, 10508,
        10509, 20107, 20307, 10310, 10605, 20407, 10010, 20507, 10406, 10210, 10011, 10407, 10408, 10409,
        20207,),
    (
        (0, (10311, 10606,)),
        (2, (10312, 10607, 10608, 10609,)),
        (3, (10012,)),
        (4, (10410,)),
        (7, (10510,)),
    ),
    (10412, 10411, 10313, 100, 10013, 200, 101, 201, 10114, 10211, 102, 202,),
    (10610, 103, 203, 10511, 10413, 104, 204,),
    (10212, 105, 205, 106, 206, 107, 207, 10213, 0, 1, 2, 10611, 3, 10512, 10513, 208, 5, 10612, 108,),
    (109, 209, 7, 110, 10613, 4, 6, 112, 111, 113, 10314, 210, 10014, 10115, 211, 8, 10, 114, 212,),
    (9, 213, 10214, 10514, 214, 10414, 10315, 12, 10015, 11, 115, 13, 215, 10215, 10515, 14, 10614, 15, 10415,
        10615,),
)


def dot(a, b):
    return jnp.dot(a, b, preferred_element_type=jnp.float32)


def dot_t(a, b):
    return lax.dot_general(a, b, (((1,), (1,)), ((), ())), preferred_element_type=jnp.float32)


def t_dot(a, b):
    return lax.dot_general(a, b, (((0,), (0,)), ((), ())), preferred_element_type=jnp.float32)


def repeat(count, body):
    def step(k, nothing):
        body(k)
        return nothing

    lax.fori_loop(0, count, step, 0)


def rows_at(k, size, base=0):
    return pl.ds(pl.multiple_of(base + k * size, 16), size)


def lanes_at(k, size, base=0):
    return pl.ds(pl.multiple_of(base + k * size, 128), size)


def rotate(u, cosine, sine):
    front, back = u[:32], u[32:]
    return jnp.concatenate([front * cosine - back * sine, front * sine + back * cosine], axis=0)


def probabilities(keys, query, limit, chunk):
    scores = t_dot(keys, query) * (HEAD_DIMENSION ** (-0.5))
    key_pos = chunk * 256 + lax.broadcasted_iota(jnp.int32, (256, 384), 0)
    return jnp.where(key_pos <= limit, jnp.exp(scores), 0.0)


def heads_wide(ref, group, lanes):
    return jnp.concatenate(
        [ref[pl.ds(pl.multiple_of(group * 192 + 64 * i, 64), 64), lanes] for i in range(3)], axis=1
    )


def three_wide(row):
    return jnp.concatenate([row] * 3, axis=1)


def forward_body(
    cat, note, x, cosine, sine, limit, gate, up, down,
    gate_w, up_w, down_w, wcat, notes, attn_in_t, hidden, query, keys_values, attn, denom,
    attn_in, raw, own_kv, weights, proj, seq_in, dp_in, own_sems, note_a, note_b, note_c, note_d, *sems
):
    place = position()
    d, s = mesh_place(*place)
    greet(place, True)
    shards = dict(zip(FFN_NAMES, (gate, up, down)))
    wholes = dict(zip(FFN_NAMES, (gate_w, up_w, down_w)))
    cat_spreads = make_spreads(place, CAT_JOBS, {"cat": cat}, {"cat": weights}, sems[:4])
    ffn_spreads = make_spreads(place, FFN_JOBS, shards, wholes, sems[4:8])
    kv_spreads = make_kv_spreads(place, own_kv, keys_values, sems[8:10])
    steps = [[spread.steps() for spread in family] for family in (cat_spreads, ffn_spreads, kv_spreads)]

    def run(tokens):
        for token in tokens:
            steps[token // 10000][token // 100 % 100][token % 100]()

    tiles = Notes(place, lambda peer: note, note, seq_in, dp_in, (note_a, note_b, note_c, note_d))
    run(FORWARD_PLAN[0])
    for k in range(1, 8):
        tiles.along_seq(k).start()
    for k in range(1, 4):
        tiles.along_dp(k).start()
    own = [
        pltpu.make_async_copy(
            shards[name], piece_of(wholes[name], (name, 0, 768 if name == "down" else 288, ""))(place), own_sems.at[k]
        )
        for k, name in enumerate(FFN_NAMES)
    ]
    for copy in own:
        copy.start()
    weights[rows_at(d, 288), lanes_at(s, 384)] = cat[...]
    for copy in own:
        copy.wait()
    run(FORWARD_PLAN[1])
    tiles.wait_seq()
    tiles.wait_dp()
    seq_in[s] = note[...]
    dp_in[d] = note[...]
    gains = seq_in[0]
    for k in range(1, 8):
        gains = gains + seq_in[k]
    notes[0:8, :] = gains
    notes[8:16, :] = dp_in[0] + dp_in[1] + dp_in[2] + dp_in[3]

    def norm(k):
        rows = rows_at(k, 32)
        part = x[rows, :].astype(jnp.float32)
        scale = lax.rsqrt(jnp.mean(part * part, axis=-1, keepdims=True) + norm_eps)
        attn_in[rows, :] = (part * scale * notes[0:1, :]).astype(jnp.bfloat16)

    repeat(8, norm)
    attn_in_t[...] = attn_in[...].T
    run(FORWARD_PLAN[2])
    for spread in cat_spreads:
        spread.wait_core()

    def project(b):
        block = dot(attn_in[...], weights[:, lanes_at(b, 384)][:, :256]).T
        raw[rows_at(b, 144), :] = block[:144]
        raw[rows_at(b, 48, 1152), :] = block[144:192]
        raw[rows_at(b, 48, 1536), :] = block[192:240]

    repeat(8, project)
    out_copy = pltpu.make_async_copy(weights, wcat, own_sems.at[3])
    out_copy.start()

    def turn(ref, rows_of):
        def one(h):
            ref[rows_at(h, 64), :] = rotate(raw[rows_of(h), :], cosine[...], sine[...]).astype(jnp.bfloat16)

        return one

    repeat(6, turn(own_kv, lambda h: rows_at(h, 64, 1152)))
    own_kv[384:768, :] = raw[1536:1920, :].astype(jnp.bfloat16)
    repeat(18, turn(query, lambda h: rows_at(h, 64)))
    run(FORWARD_PLAN[3])
    here = lanes_at(s, 128)
    for slot in range(2):
        keys_values[slot, :, here] = own_kv[:, slot * 128: slot * 128 + 128]
    run(FORWARD_PLAN[4])

    def attend(slot, group):
        lanes = lanes_at(slot, 128)
        bound = three_wide(limit[:, lanes])
        wide = heads_wide(query, group, lanes)

        def one_chunk(chunk, carry):
            total, numer = carry
            cols = lanes_at(chunk, 256)
            expo = probabilities(keys_values[slot, rows_at(group, 64), cols], wide, bound, chunk)
            total = total + jnp.sum(expo, axis=0, keepdims=True)
            numer = numer + dot(keys_values[slot, rows_at(group, 64, 384), cols], expo.astype(jnp.bfloat16))
            return (total, numer)

        total, numer = lax.fori_loop(
            0, 4, one_chunk, (jnp.zeros((1, 384), jnp.float32), jnp.zeros((64, 384), jnp.float32)), unroll=True
        )
        mean = numer / total
        for i in range(3):
            attn[pl.ds(pl.multiple_of(group * 192 + 64 * i, 64), 64), lanes] = mean[:, i * 128: i * 128 + 128]
        denom[group, 0:3, lanes] = jnp.concatenate([total[:, i * 128: i * 128 + 128] for i in range(3)], axis=0)

    def unit(k):
        attend(k // 6, lax.rem(k, 6))
        for at, tokens in FORWARD_PLAN[5]:
            pl.when(k == at)(lambda tokens=tokens: run(tokens))

    repeat(12, unit)

    def out_project(b):
        block = t_dot(attn[...].astype(jnp.bfloat16), weights[:, lanes_at(b, 384)][:, 128:]).T
        proj[rows_at(b, 144), :] = block[112:256]

    repeat(8, out_project)
    hidden[...] = x[...].astype(jnp.float32) + proj[...].T
    run(FORWARD_PLAN[6])
    for spread in cat_spreads + ffn_spreads + kv_spreads:
        spread.finish()
    for spread in ffn_spreads:
        spread.wait_core()
    for k in range(1, 8):
        tiles.along_seq(k).wait_send()
    for k in range(1, 4):
        tiles.along_dp(k).wait_send()
    out_copy.wait()


def forward_call(cat, note, x, cosine, sine, limit, gate, up, down):
    vmem, anywhere = pl.BlockSpec(memory_space=pltpu.VMEM), pl.BlockSpec(memory_space=pl.ANY)
    return pl.pallas_call(
        forward_body,
        out_shape=[jax.ShapeDtypeStruct((1152, 3072), jnp.bfloat16)] * 4
        + [
            jax.ShapeDtypeStruct((16, 1152), jnp.float32),
            jax.ShapeDtypeStruct((1152, 256), jnp.bfloat16),
            jax.ShapeDtypeStruct((256, 1152), jnp.float32),
            jax.ShapeDtypeStruct((1152, 256), jnp.bfloat16),
            jax.ShapeDtypeStruct((2, 768, 1024), jnp.bfloat16),
            jax.ShapeDtypeStruct((1152, 256), jnp.float32),
            jax.ShapeDtypeStruct((6, 8, 256), jnp.float32),
        ],
        in_specs=[vmem] * 9,
        out_specs=[anywhere] * 4 + [vmem] * 7,
        scratch_shapes=[
            pltpu.VMEM((256, 1152), jnp.bfloat16),
            pltpu.VMEM((1920, 256), jnp.float32),
            pltpu.VMEM((768, 256), jnp.bfloat16),
            pltpu.VMEM((1152, 3072), jnp.bfloat16),
            pltpu.VMEM((1152, 256), jnp.float32),
            pltpu.VMEM((8, 8, 1152), jnp.float32),
            pltpu.VMEM((4, 8, 1152), jnp.float32),
            pltpu.SemaphoreType.DMA((4,)),
        ]
        + NOTE_SEMS
        + spread_sems(CAT_JOBS)
        + spread_sems(FFN_JOBS)
        + spread_sems(KV_JOBS)[:2],
        compiler_params=pltpu.CompilerParams(
            collective_id=3, has_side_effects=True, vmem_limit_bytes=48 * 1024 * 1024
        ),
        name="attention_forward",
    )(cat, note, x, cosine, sine, limit, gate, up, down)


def backward_body(
    grad_hidden, attn_in_t, wcat, keys_values, query, attn, denom, cosine, sine, limit, x, scales, small,
    grad_gate, grad_up, grad_down,
    own_gate, own_up, own_down, own_cat, grad_tokens, totals, grad_cat,
    weights, whole_kv, part_kv, turned, total, own_kv, left, grad_t, note, seq_in, dp_in, row_sum,
    load, store, kv_send, kv_recv, kv_arrived, note_a, note_b, note_c, note_d, *scratch
):
    place = position()
    d, s = mesh_place(*place)
    greet(place, True)
    sums = dict(zip(FFN_NAMES, (grad_gate, grad_up, grad_down)))
    owned = dict(zip(FFN_NAMES, (own_gate, own_up, own_down)))
    split = len(fold_scratch(FOLD_FFN, False))
    folds = [
        JobFold(place, job, j, sums[job[0]], owned[job[0]], scratch[:split], False) for j, job in enumerate(FOLD_FFN)
    ]
    cat_folds = [JobFold(place, job, j, grad_cat, own_cat, scratch[split:], True) for j, job in enumerate(FOLD_CAT)]
    tiles = Notes(place, lambda peer: note, row_sum, seq_in, dp_in, (note_a, note_b, note_c, note_d))

    def kv_fold(j, slot, row, order):
        def out(value):
            own_kv[row: row + 256, slot * 128: slot * 128 + 128] = value

        spot = kv_spot(part_kv, slot, row)
        return Fold(place, order, lambda who: spot(who), kv_arrived.at[j], (kv_send, kv_recv), j, out, kv_amount(part_kv))

    kv_folds = [kv_fold(j, *job) for j, job in enumerate(FOLD_KV)]
    steps = [
        [fold.fold.steps() for fold in cat_folds],
        [fold.fold.steps() for fold in folds],
        [fold.steps() for fold in kv_folds],
    ]

    def run(tokens):
        for token in tokens:
            steps[token // 10000][token // 100 % 100][token % 100]()

    for dy in (1, 0):
        for fold in folds:
            fold.begin(dy)

    def block_load(b):
        return pltpu.make_async_copy(wcat.at[:, lanes_at(b, 384)], weights.at[:, lanes_at(b, 384)], load.at[b])

    repeat(8, lambda b: block_load(b).start())
    kv_in = pltpu.make_async_copy(keys_values, whole_kv, load.at[8])
    kv_in.start()
    grad_t[...] = grad_hidden[...].T.astype(jnp.bfloat16)
    total[...] = jnp.zeros_like(total)

    def out_rows(b):
        return jnp.concatenate([jnp.zeros((112, 256), jnp.bfloat16), grad_t[rows_at(b, 144), :]], axis=0)

    def out_back(b):
        block_load(b).wait()
        total[...] += dot(weights[:, lanes_at(b, 384)][:, 128:], out_rows(b))

    repeat(8, out_back)
    run(BACKWARD_PLAN[0])
    kv_in.wait()
    scale = HEAD_DIMENSION ** (-0.5)

    def attend_back(slot, group):
        lanes = lanes_at(slot, 128)
        bound = three_wide(limit[:, lanes])
        wide = heads_wide(query, group, lanes)
        grads, ratios = [], []
        for i in range(3):
            rows = pl.ds(pl.multiple_of(group * 192 + 64 * i, 64), 64)
            grad = total[rows, lanes].astype(jnp.bfloat16).astype(jnp.float32)
            bottom = denom[group, i: i + 1, lanes]
            ratios.append(jnp.sum(grad * attn[rows, lanes], axis=0, keepdims=True) / bottom)
            grads.append((grad / bottom).astype(jnp.bfloat16))
        grads, ratios = jnp.concatenate(grads, axis=1), jnp.concatenate(ratios, axis=1)

        def one_chunk(chunk, sum_query):
            cols = lanes_at(chunk, 256)
            keys = whole_kv[slot, rows_at(group, 64), cols]
            values = whole_kv[slot, rows_at(group, 64, 384), cols]
            expo = probabilities(keys, wide, bound, chunk)
            grad_prob = t_dot(values, grads)
            grad_score = (expo * (grad_prob - ratios)).astype(jnp.bfloat16)
            part_kv[slot, rows_at(group, 64), cols] = (dot_t(wide, grad_score) * scale).astype(jnp.bfloat16)
            part_kv[slot, rows_at(group, 64, 384), cols] = dot_t(grads, expo.astype(jnp.bfloat16)).astype(jnp.bfloat16)
            return sum_query + dot(keys, grad_score)

        sum_query = lax.fori_loop(0, 4, one_chunk, jnp.zeros((64, 384), jnp.float32), unroll=True) * scale
        for i in range(3):
            total[pl.ds(pl.multiple_of(group * 192 + 64 * i, 64), 64), lanes] = sum_query[:, i * 128: i * 128 + 128]

    def unit(k):
        attend_back(k // 6, lax.rem(k, 6))
        for at, tokens in BACKWARD_PLAN[1]:
            pl.when(k == at)(lambda tokens=tokens: run(tokens))

    repeat(12, unit)
    run(BACKWARD_PLAN[2])

    def turn_back(ref, source, count):
        def one(h):
            rows = rows_at(h, 64)
            ref[rows, :] = rotate(source[rows, :], cosine[...], -sine[...]).astype(ref.dtype)

        repeat(count, one)

    turn_back(turned, total, 18)
    turn_back(own_kv, own_kv, 6)
    total[...] = jnp.zeros_like(total)

    def last_block(b):
        rows = jnp.concatenate(
            [
                turned[rows_at(b, 144), :],
                own_kv[rows_at(b, 48), :].astype(jnp.bfloat16),
                own_kv[rows_at(b, 48, 384), :].astype(jnp.bfloat16),
                jnp.zeros((16, 256), jnp.bfloat16),
            ],
            axis=0,
        )
        total[...] += dot(weights[:, lanes_at(b, 384)][:, :256], rows)
        slot = lax.rem(b, 2)
        out = pltpu.make_async_copy(left.at[slot], grad_cat.at[:, lanes_at(b, 384)], store.at[slot])
        pl.when(b >= 2)(lambda: out.wait())
        grad = dot_t(attn_in_t[...], rows)
        out_grad = dot_t(attn[...].astype(jnp.bfloat16), out_rows(b))
        left[slot, :, 0:128] = grad[:, :128].astype(jnp.bfloat16)
        left[slot, :, 128:256] = (grad[:, 128:] + out_grad[:, :128]).astype(jnp.bfloat16)
        left[slot, :, 256:384] = out_grad[:, 128:].astype(jnp.bfloat16)
        out.start()
        for at, tokens in BACKWARD_PLAN[3]:
            pl.when(b == at)(lambda tokens=tokens: run(tokens))

    repeat(8, last_block)
    for slot in range(2):
        pltpu.make_async_copy(left.at[slot], grad_cat.at[:, pl.ds((6 + slot) * 384, 384)], store.at[slot]).wait()
    for dy in (1, 0):
        for fold in cat_folds:
            fold.begin(dy)
    run(BACKWARD_PLAN[4])
    grad_tokens[...] = total[...].T
    note[...] = small[...]

    def finish_rows(k):
        rows = rows_at(k, 32)
        grad = grad_tokens[rows, :]
        scale_in = scales[rows, 0:1]
        normed = x[rows, :].astype(jnp.float32) * scale_in
        note[0:1, :] += jnp.sum(grad * normed, axis=0, keepdims=True)
        grad = grad * small[3:4, :]
        inner = grad - normed * jnp.mean(grad * normed, axis=-1, keepdims=True)
        grad_tokens[rows, :] = grad_hidden[rows, :] + scale_in * inner

    repeat(8, finish_rows)
    run(BACKWARD_PLAN[5])
    for k in range(1, 8):
        tiles.along_seq(k).start()
    run(BACKWARD_PLAN[6])
    tiles.wait_seq()
    seq_in[s] = note[...]
    along = seq_in[0]
    for k in range(1, 8):
        along = along + seq_in[k]
    row_sum[...] = along
    run(BACKWARD_PLAN[7])
    for k in range(1, 4):
        tiles.along_dp(k).start()
    run(BACKWARD_PLAN[8])
    tiles.wait_dp()
    dp_in[d] = row_sum[...]
    totals[...] = dp_in[0] + dp_in[1] + dp_in[2] + dp_in[3]
    for fold in folds + kv_folds + cat_folds:
        fold.finish()
    for k in range(1, 8):
        tiles.along_seq(k).wait_send()
    for k in range(1, 4):
        tiles.along_dp(k).wait_send()


def backward_call(
    grad_hidden, attn_in_t, wcat, keys_values, query, attn, denom, cosine, sine, limit, x, scales, small,
    grad_gate, grad_up, grad_down
):
    vmem, anywhere = pl.BlockSpec(memory_space=pltpu.VMEM), pl.BlockSpec(memory_space=pl.ANY)
    jobs = len(KV_JOBS)
    most = max(fold_slots(order)[1] for _, _, order in FOLD_KV)
    return pl.pallas_call(
        backward_body,
        out_shape=[
            jax.ShapeDtypeStruct((288, 384), jnp.float32),
            jax.ShapeDtypeStruct((288, 384), jnp.float32),
            jax.ShapeDtypeStruct((144, 768), jnp.float32),
            jax.ShapeDtypeStruct((288, 384), jnp.float32),
            jax.ShapeDtypeStruct((256, 1152), jnp.float32),
            jax.ShapeDtypeStruct((8, 1152), jnp.float32),
            jax.ShapeDtypeStruct((1152, 3072), jnp.bfloat16),
        ],
        in_specs=[vmem, vmem, anywhere, anywhere] + [vmem] * 9 + [anywhere] * 3,
        out_specs=[vmem] * 6 + [anywhere],
        scratch_shapes=[
            pltpu.VMEM((1152, 3072), jnp.bfloat16),
            pltpu.VMEM((2, 768, 1024), jnp.bfloat16),
            pltpu.VMEM((2, 768, 1024), jnp.bfloat16),
            pltpu.VMEM((1152, 256), jnp.bfloat16),
            pltpu.VMEM((1152, 256), jnp.float32),
            pltpu.VMEM((768, 256), jnp.float32),
            pltpu.VMEM((2, 1152, 384), jnp.bfloat16),
            pltpu.VMEM((1152, 256), jnp.bfloat16),
            pltpu.VMEM((8, 1152), jnp.float32),
            pltpu.VMEM((8, 8, 1152), jnp.float32),
            pltpu.VMEM((4, 8, 1152), jnp.float32),
            pltpu.VMEM((8, 1152), jnp.float32),
            pltpu.SemaphoreType.DMA((9,)),
            pltpu.SemaphoreType.DMA((2,)),
            pltpu.SemaphoreType.DMA((jobs,)),
            pltpu.SemaphoreType.DMA((jobs, most)),
            pltpu.VMEM((jobs, most, 256, 128), jnp.bfloat16),
        ]
        + NOTE_SEMS
        + fold_scratch(FOLD_FFN, False)
        + fold_scratch(FOLD_CAT, True),
        compiler_params=pltpu.CompilerParams(
            collective_id=4, has_side_effects=True, vmem_limit_bytes=VMEM_MOST
        ),
        name="attention_backward",
    )(
        grad_hidden, attn_in_t, wcat, keys_values, query, attn, denom, cosine, sine, limit, x, scales, small,
        grad_gate, grad_up, grad_down,
    )


def per_device_fast(
    tokens, teacher, lengths, w_query, key_weight, value_weight, w_out, w_gate, w_up, w_down, gain_attn, gain_ffn
):
    slots, part, width = tokens.shape
    rows = slots * part
    total_tokens = slots * lax.axis_size("dp") * part * lax.axis_size("seq")
    positions = lax.axis_index("seq") * part + jnp.arange(part, dtype=jnp.int32)
    cosine, sine = rope_tables(positions, HEAD_DIMENSION)
    cosine_t = jnp.concatenate([cosine.T] * slots, axis=1)
    sine_t = jnp.concatenate([sine.T] * slots, axis=1)
    limit = jnp.minimum(positions[None, :], lengths[:, None] - 1).reshape(1, rows)
    note = lax.dynamic_update_slice(
        jnp.zeros((8, width), jnp.float32),
        jnp.stack([gain_attn, gain_ffn]).astype(jnp.float32),
        (0, lax.axis_index("seq") * gain_attn.shape[0]),
    )
    note = note.at[2].set(jnp.sum(lengths).astype(jnp.float32))
    x_b = tokens.reshape(rows, width)
    gate_w, up_w, down_t, cat, notes, attn_in_t, hidden, query, keys_values, attn, denom = forward_call(
        jnp.concatenate([w_query, key_weight, value_weight, w_out], axis=1),
        note, x_b, cosine_t, sine_t, limit, w_gate, w_up, w_down.T,
    )
    gain_a, gain_f = notes[0:1], notes[1:2]
    count = notes[10, 0]
    factor = total_tokens / count
    r2 = lax.rsqrt(jnp.mean(hidden * hidden, axis=-1, keepdims=True) + norm_eps)
    n2 = hidden * r2
    ffn_in = (n2 * gain_f).astype(jnp.bfloat16)
    gate = dot(ffn_in, gate_w)
    up = dot(ffn_in, up_w)
    sig = jax.nn.sigmoid(gate)
    hid = (gate * sig * up).astype(jnp.bfloat16)
    valid = (positions[None, :] < lengths[:, None]).reshape(rows, 1)
    out_f = jnp.where(valid, hidden + dot_t(hid, down_t), 0.0)
    diff = jnp.where(valid, out_f - teacher.reshape(rows, width).astype(jnp.float32), 0.0)
    squares = jnp.sum(diff * diff)
    cot = factor * diff
    cot_b = cot.astype(jnp.bfloat16)
    grad_hid = dot(cot_b, down_t)
    grad_gate_b = (grad_hid * up * sig * (1.0 + gate * (1.0 - sig))).astype(jnp.bfloat16)
    grad_up_b = (grad_hid * gate * sig).astype(jnp.bfloat16)
    core = lax.rem(lax.axis_index("dp"), 2)

    def swap(value):
        return lax.ppermute(value, "dp", [(0, 1), (1, 0), (2, 3), (3, 2)])

    def lane(value, which):
        parts = value.reshape(rows, 2, 2, value.shape[1] // 4)
        return lax.dynamic_index_in_dim(parts, which, 2, keepdims=False).reshape(rows, -1)

    def over_cores(value):
        return jnp.concatenate([value, swap(value)], axis=0)

    def lane_over_cores(value):
        return jnp.concatenate([lane(value, core), swap(lane(value, 1 - core))], axis=0)

    ffn_lane = lane_over_cores(ffn_in)
    grad_down_t = t_dot(over_cores(cot_b), lane_over_cores(hid)).astype(jnp.bfloat16)
    grad_gate_w = t_dot(ffn_lane, over_cores(grad_gate_b)).astype(jnp.bfloat16)
    grad_up_w = t_dot(ffn_lane, over_cores(grad_up_b)).astype(jnp.bfloat16)
    grad_ffn_in = dot_t(grad_gate_b, gate_w) + dot_t(grad_up_b, up_w)
    part_gain_f = jnp.sum(grad_ffn_in * n2, axis=0)
    gn = grad_ffn_in * gain_f
    grad_hidden = cot + r2 * (gn - n2 * jnp.mean(gn * n2, axis=-1, keepdims=True))
    x = x_b.astype(jnp.float32)
    r1 = lax.rsqrt(jnp.mean(x * x, axis=-1, keepdims=True) + norm_eps)
    small = jnp.concatenate(
        [
            jnp.zeros((1, width), jnp.float32),
            part_gain_f[None, :],
            jnp.broadcast_to(squares, (1, width)),
            gain_a,
            jnp.zeros((4, width), jnp.float32),
        ],
        axis=0,
    )
    own_gate, own_up, own_down_t, own_cat, grad_tokens, totals, _ = backward_call(
        grad_hidden, attn_in_t, cat, keys_values, query, attn, denom, cosine_t, sine_t, limit,
        x_b, jnp.broadcast_to(r1, (rows, 128)), small, grad_gate_w, grad_up_w, grad_down_t,
    )
    own_gains = lax.dynamic_slice(
        totals, (0, lax.axis_index("seq") * gain_attn.shape[0]), (2, gain_attn.shape[0])
    )
    return (
        out_f.astype(jnp.bfloat16).reshape(tokens.shape),
        totals[2, 0] / count,
        grad_tokens.reshape(tokens.shape),
        own_cat[:, :144],
        own_cat[:, 144:192],
        own_cat[:, 192:240],
        own_cat[:, 240:],
        own_gate,
        own_up,
        own_down_t.T,
        own_gains[0],
        own_gains[1],
    )


def solution(mesh):
    placed = (
        P("dp", "seq", None),
        P("dp", "seq", None),
        P("dp"),
        P("dp", "seq"),
        P("dp", "seq"),
        P("dp", "seq"),
        P("dp", "seq"),
        P("dp", "seq"),
        P("dp", "seq"),
        P("dp", "seq"),
        P("seq"),
        P("seq"),
    )
    fits = mesh.shape["dp"] == 4 and mesh.shape["seq"] == 8
    return jax.shard_map(
        per_device_fast if fits else per_device,
        mesh=mesh,
        in_specs=placed,
        out_specs=(
            P("dp", "seq", None),
            P(),
            P("dp", "seq", None),
            P("dp", "seq"),
            P("dp", "seq"),
            P("dp", "seq"),
            P("dp", "seq"),
            P("dp", "seq"),
            P("dp", "seq"),
            P("dp", "seq"),
            P("seq"),
            P("seq"),
        ),
        check_vma=False,
    )
```

profile of v0, /device:TPU:0, one launch (start us, length us, event | category | flops | bytes accessed | tf_op | source)
XLA Modules:
  0.0 403.5 jit_solution(6635110062070209201)
XLA Ops:
  0.7 1.1 copy.35
  3.6 1.0 copy.32
  5.9 1.3 broadcast_add_fusion
  9.7 148.9 %attention_forward.1 = (bf16[1152,3072]{1,0:T(8,128)(2,1)}, bf16[1152,3072]{1,0:T(8,128)(2,1)}, bf16[1152,3072]{1,0:T(8,128)(2,1)}, bf16[1152,3072]{1,0:T(8,128)...) custom-call(bf16[288,384]{1,0:T(8,128)(2,1)S(1)} %pad_maximum_fusion, ...), custom_call_target="tpu_custom_call" | custom-call | tf_op jit(solution)/shard_map/attention_forward/pallas_call | solution.py:1248
  161.1 5.4 %fusion.22 = f32[256,3072]{1,0:T(8,128)S(1)} fusion(bf16[256,1152]{1,0:T(8,128)(2,1)S(1)} %multiply_convert_fusion.3, bf16[1152,3072]{1,0:T(8,128)(2,1)} %get-tuple-element.43), kind=kOutput, calls=%fused_computation.61 | convolution fusion | flops 1811939328 | bytes 10813440 | tf_op jit(solution)/shard_map/dot_general | solution.py:1068
  166.6 2.7 multiply_convert_fusion.2
  169.3 3.7 multiply_convert_fusion.4
  173.3 5.9 %multiply_convert_fusion = (bf16[256,3072]{1,0:T(8,128)(2,1)}, bf16[256,3072]{1,0:T(8,128)(2,1)}) fusion(f32[256,3072]{1,0:T(8,128)S(1)} %fusion.22, f32[256,3072]{1,0:T(8,128)S(1)} %get-tuple-element.106, bf16[256,1152]{1,0:T(8,128)(2,1)} %get-tuple-element.107, bf16[1152,3072]{1,0:T(8,128)(2,1)S(1)} %bitcast.60), kind=kOutput, calls=%fused_computation.9 | convolution fusion | flops 1822162944 | bytes 17104896 | tf_op jit(solution)/shard_map/dot_general | solution.py:1068
  181.1 4.2 %reshape.175 = bf16[256,2,2,768]{3,2,1,0:T(2,128)(2,1)S(1)} reshape(bf16[256,3072]{1,0:T(8,128)(2,1)} %copy-done.12) | data formatting | bytes 3145728 | tf_op jit(solution)/shard_map/reshape | solution.py:1560
  185.3 4.9 %constant_dynamic-slice_fusion.2 = (bf16[256,2,1,768]{3,2,1,0:T(2,128)(2,1)}, bf16[256,2,1,768]{3,2,1,0:T(2,128)(2,1)}) fusion(bf16[256,2,2,768]{3,2,1,0:T(2,128)(2,1)S(1)} %reshape.175, s32[]{:T(128)S(6)} %select_n.24, s32[]{:T(128)S(6)} %select_n.25), kind=kLoop, calls=%fused_computation.42 | loop fusion | bytes 3145736 | tf_op jit(solution)/shard_map/jit(dynamic_index_in_dim)/dynamic_slice | solution.py:1561
  190.2 3.4 copy.44
  194.1 5.9 %fusion.23 = f32[256,1152]{1,0:T(8,128)S(1)} fusion(bf16[256,3072]{1,0:T(8,128)(2,1)} %get-tuple-element.85, bf16[1152,3072]{1,0:T(8,128)(2,1)} %get-tuple-element.43), kind=kOutput, calls=%fused_computation.62 | convolution fusion | flops 1811939328 | bytes 9830400 | tf_op jit(solution)/shard_map/dot_general | solution.py:1072
  200.1 2.6 multiply_reduce_fusion.1
  203.0 2.5 multiply_reduce_fusion
  205.5 1.8 copy.43
  208.6 5.4 %convolution_convert_fusion.grad_down = bf16[1152,1536]{1,0:T(8,128)(2,1)} fusion(bf16[256,1536]{0,1:T(8,128)(2,1)} %collective-permute-done.4, bf16[256,1536]{0,1:T(8,128)(2,1)S(1)} %bitcast.48, bf16[256,1152]{1,0:T(8,128)(2,1)} %collective-permute-done.3, bf16[256,1152]{1,0:T(8,128)(2,1)} %get-tuple-element.107), kind=kOutput, calls=%fused_computation | convolution fusion | flops 1819213824 | bytes 6291456 | tf_op jit(solution)/shard_map/dot_general | solution.py:1076
  214.0 5.9 %convolution_convert_fusion.2.grad_gate = bf16[576,3072]{1,0:T(8,128)(2,1)} fusion(bf16[256,3072]{1,0:T(8,128)(2,1)} %collective-permute-done.1, bf16[256,3072]{1,0:T(8,128)(2,1)} %get-tuple-element.85, bf16[256,576]{0,1:T(8,128)(2,1)} %collective-permute-done, bf16[256,576]{0,1:T(8,128)(2,1)S(1)} %bitcast.51), kind=kOutput, calls=%fused_computation.2 | convolution fusion | flops 1821179904 | bytes 7274496 | tf_op jit(solution)/shard_map/dot_general | solution.py:1076
  219.9 5.3 %convolution_convert_fusion.1.grad_up = bf16[576,3072]{1,0:T(8,128)(2,1)} fusion(bf16[256,3072]{1,0:T(8,128)(2,1)} %collective-permute-done.2, bf16[256,3072]{1,0:T(8,128)(2,1)S(1)} %copy-done.29, bf16[256,576]{0,1:T(8,128)(2,1)} %collective-permute-done, bf16[256,576]{0,1:T(8,128)(2,1)S(1)} %bitcast.52), kind=kOutput, calls=%fused_computation.1 | convolution fusion | flops 1821179904 | bytes 7274496 | tf_op jit(solution)/shard_map/dot_general | solution.py:1076
  226.0 163.3 %attention_backward.1 = (f32[288,384]{1,0:T(8,128)}, f32[288,384]{1,0:T(8,128)}, f32[144,768]{1,0:T(8,128)}, f32[288,384]{1,0:T(8,128)}, f32[256,1152]{1,0:T(8,1...) custom-call(f32[256,1152]{1,0:T(8,128)} %get-tuple-element.87.grad_hidden, bf16[1152,256]{1,0:T(8,128)(2,1)} %copy-done.2, ...), custom_call_target="tpu_custom_call" | custom-call | tf_op jit(solution)/shard_map/attention_backward/pallas_call | solution.py:1468
  389.4 1.3 fusion.18
  390.7 1.1 fusion.19
  391.8 1.2 slice.48
  397.5 1.4 fusion.21
  398.9 1.0 copy.51
  (125 shorter events, 16.9 us)
Async XLA Ops:
  0.6 9.0 %copy-start = (bf16[2,128,1152]{2,1,0:T(8,128)(2,1)S(1)}, bf16[2,128,1152]{2,1,0:T(8,128)(2,1)}, u32[]{:S(2)}) copy-start(bf16[2,128,1152]{2,1,0:T(8,128)(2,1)} %param.14) | copy-start | bytes 1769476
  0.7 9.0 %copy-start.6 = (bf16[288,384]{1,0:T(8,128)(2,1)S(1)}, bf16[288,384]{1,0:T(8,128)(2,1)}, u32[]{:S(2)}) copy-start(bf16[288,384]{1,0:T(8,128)(2,1)} %gate.1) | copy-start | bytes 663556
  0.7 9.0 %copy-start.7 = (bf16[288,384]{1,0:T(8,128)(2,1)S(1)}, bf16[288,384]{1,0:T(8,128)(2,1)}, u32[]{:S(2)}) copy-start(bf16[288,384]{1,0:T(8,128)(2,1)} %up.1) | copy-start | bytes 663556
  0.7 9.0 %copy-start.8 = (bf16[768,144]{0,1:T(8,128)(2,1)S(1)}, bf16[768,144]{0,1:T(8,128)(2,1)}, u32[]{:S(2)}) copy-start(bf16[768,144]{0,1:T(8,128)(2,1)} %param.23) | copy-start | bytes 663556
  8.0 152.1 %copy-start.4 = (f32[32,256]{1,0:T(8,128)}, f32[32,256]{1,0:T(8,128)S(1)}, u32[]{:S(2)}) copy-start(f32[32,256]{1,0:T(8,128)S(1)} %pad_maximum_fusion.4.cosine) | copy-start | bytes 98308
  8.1 152.1 %copy-start.5 = (f32[32,256]{1,0:T(8,128)}, f32[32,256]{1,0:T(8,128)S(1)}, u32[]{:S(2)}) copy-start(f32[32,256]{1,0:T(8,128)S(1)} %pad_maximum_fusion.5.sine) | copy-start | bytes 98308
  8.8 160.5 %copy-start.26 = (pred[256]{0:T(512)(128)(4,1)}, pred[256]{0:T(512)(128)(4,1)S(1)}, u32[]{:S(2)}) copy-start(pred[256]{0:T(512)(128)(4,1)S(1)} %compare_bitcast_fusion) | copy-start | bytes 772
  8.9 151.3 %copy-start.10 = (s32[2,128]{1,0:T(2,128)}, s32[2,128]{1,0:T(2,128)S(1)}, u32[]{:S(2)}) copy-start(s32[2,128]{1,0:T(2,128)S(1)} %broadcast_minimum_fusion) | copy-start | bytes 3076
  158.6 7.9 %copy-start.1 = (f32[1152,256]{1,0:T(8,128)}, f32[1152,256]{1,0:T(8,128)S(1)}, u32[]{:S(2)}) copy-start(f32[1152,256]{1,0:T(8,128)S(1)} %get-tuple-element.50.attn) | copy-start | bytes 3538948
  158.6 7.9 %copy-start.2 = (bf16[1152,256]{1,0:T(8,128)(2,1)}, bf16[1152,256]{1,0:T(8,128)(2,1)S(1)}, u32[]{:S(2)}) copy-start(bf16[1152,256]{1,0:T(8,128)(2,1)S(1)} %get-tuple-element.46.attn_in_t) | copy-start | bytes 1769476
  158.6 7.9 %copy-start.3 = (bf16[1152,256]{1,0:T(8,128)(2,1)}, bf16[1152,256]{1,0:T(8,128)(2,1)S(1)}, u32[]{:S(2)}) copy-start(bf16[1152,256]{1,0:T(8,128)(2,1)S(1)} %get-tuple-element.49.query) | copy-start | bytes 1769476
  158.6 7.9 %copy-start.9 = (f32[6,8,256]{2,1,0:T(8,128)}, f32[6,8,256]{2,1,0:T(8,128)S(1)}, u32[]{:S(2)}) copy-start(f32[6,8,256]{2,1,0:T(8,128)S(1)} %get-tuple-element.51.denom) | copy-start | bytes 147460
  160.0 6.5 %copy-start.21 = (f32[1152]{0:T(1024)}, f32[1152]{0:T(1024)S(1)}, u32[]{:S(2)}) copy-start(f32[1152]{0:T(1024)S(1)} %get-tuple-element.98) | copy-start | bytes 13828
  161.1 8.2 %slice-start.4 = ((s8[7077888]{0:T(1024)(128)(4,1)}), s8[4194304]{0:T(1024)(128)(4,1)S(1)}, s32[]{:S(2)}) async-start(s8[7077888]{0:T(1024)(128)(4,1)} %bitcast.59), calls=%async_computation.4 | async-start | bytes 8388608
  173.0 35.6 %collective-permute-start.3 = (bf16[256,1152]{1,0:T(8,128)(2,1)}, bf16[256,1152]{1,0:T(8,128)(2,1)}, u32[]{:S(2)}, u32[]{:S(2)}) collective-permute-start(bf16[256,1152]{1,0:T(8,128)(2,1)} %get-tuple-element.107), channel_id=1, source_target_pairs={{0,8},{8,0},{16,24},{24,16},{1,9},{9,1},{17,25},{25,17},{2,10},{10... | collective-permute-start | bytes 1769480 | tf_op jit(solution)/shard_map/ppermute | solution.py:1557
  179.3 34.7 %collective-permute-start.1 = (bf16[256,3072]{1,0:T(8,128)(2,1)}, bf16[256,3072]{1,0:T(8,128)(2,1)}, u32[]{:S(2)}, u32[]{:S(2)}) collective-permute-start(bf16[256,3072]{1,0:T(8,128)(2,1)} %get-tuple-element.85), channel_id=1, source_target_pairs={{0,8},{8,0},{16,24},{24,16},{1,9},{9,1},{17,25},{25,17},{2,10},{10... | collective-permute-start | bytes 4718600 | tf_op jit(solution)/shard_map/ppermute | solution.py:1557
  180.5 33.5 %collective-permute-start = (bf16[256,576]{0,1:T(8,128)(2,1)}, bf16[256,576]{0,1:T(8,128)(2,1)}, u32[]{:S(2)}, u32[]{:S(2)}) collective-permute-start(bf16[256,576]{0,1:T(8,128)(2,1)} %bitcast.10), channel_id=1, source_target_pairs={{0,8},{8,0},{16,24},{24,16},{1,9},{9,1},{17,25},{25,17},{2,10},{10... | collective-permute-start | bytes 884744 | tf_op jit(solution)/shard_map/ppermute | solution.py:1557
  180.9 39.0 %collective-permute-start.2 = (bf16[256,3072]{1,0:T(8,128)(2,1)}, bf16[256,3072]{1,0:T(8,128)(2,1)}, u32[]{:S(2)}, u32[]{:S(2)}) collective-permute-start(bf16[256,3072]{1,0:T(8,128)(2,1)} %get-tuple-element.84), channel_id=1, source_target_pairs={{0,8},{8,0},{16,24},{24,16},{1,9},{9,1},{17,25},{25,17},{2,10},{10... | collective-permute-start | bytes 4718600 | tf_op jit(solution)/shard_map/ppermute | solution.py:1557
  193.6 6.4 %slice-start.2 = ((s8[7077888]{0:T(1024)(128)(4,1)}), s8[4194304]{0:T(1024)(128)(4,1)S(1)}, s32[]{:S(2)}) async-start(s8[7077888]{0:T(1024)(128)(4,1)} %bitcast.57), calls=%async_computation.2 | async-start | bytes 8388608
  193.6 6.4 %copy-start.22 = (f32[1152]{0:T(1024)S(1)}, f32[1152]{0:T(1024)}, u32[]{:S(2)}) copy-start(f32[1152]{0:T(1024)} %copy-done.21) | copy-start | bytes 13828
  193.6 6.4 %copy-start.25 = (f32[256]{0:T(256)S(1)}, f32[256]{0:T(256)}, u32[]{:S(2)}) copy-start(f32[256]{0:T(256)} %copy-done.24) | copy-start | bytes 3076
  193.7 6.4 %slice-start.3 = ((s8[7077888]{0:T(1024)(128)(4,1)}), s8[2883584]{0:T(1024)(128)(4,1)S(1)}, s32[]{:S(2)}) async-start(s8[7077888]{0:T(1024)(128)(4,1)} %bitcast.57), calls=%async_computation.3 | async-start | bytes 5767168
  193.7 15.0 %collective-permute-start.4 = (bf16[256,1536]{0,1:T(8,128)(2,1)S(1)}, bf16[256,1536]{0,1:T(8,128)(2,1)}, u32[]{:S(2)}, u32[]{:S(2)}) collective-permute-start(bf16[256,1536]{0,1:T(8,128)(2,1)S(1)} %bitcast.47), channel_id=1, source_target_pairs={{0,8},{8,0},{16,24},{24,16},{1,9},{9,1},{17,25},{25,17},{2,10},{10... | collective-permute-start | bytes 2359304 | tf_op jit(solution)/shard_map/ppermute | solution.py:1557
  389.4 9.5 %copy-start.13 = (f32[256,1152]{1,0:T(8,128)S(1)}, f32[256,1152]{1,0:T(8,128)}, u32[]{:S(2)}) copy-start(f32[256,1152]{1,0:T(8,128)} %get-tuple-element.53) | copy-start | bytes 3538948
  (17 other events, 66.3 us)
where the time goes:
time: 409 us; the launch traced here: 404 us
  Pallas kernels  312 us (76%)
  matrix products  42.8 us (10%)
  local copies, waits for them, and re-layouts  36.2 us (9%)
  other arithmetic  5.52 us (1%)
  between operations  5.38 us (1%)
    pallas_call x1, Pallas kernels, backward_call(): pl.pallas_call(backward_body, out_shape=[jax.ShapeDtypeStruct((288, 384),...  163 us
    pallas_call x1, Pallas kernels, forward_call(): pl.pallas_call(forward_body, out_shape=[jax.ShapeDtypeStruct((1152, 3072)...  149 us
    dot_general x3, matrix products, t_dot(): lax.dot_general(a, b, (((0,), (0,)), ((), ())), preferred_element_type=jn...  16.6 us
    unnamed x86, local copies, waits for them, and re-layouts  15.7 us
    dot_general x3, matrix products, dot(): return jnp.dot(a, b, preferred_element_type=jnp.float32)  14 us
    dot_general x3, matrix products, dot_t(): lax.dot_general(a, b, (((1,), (1,)), ((), ())), preferred_element_type=jn...  12.2 us
  transfers between devices with their start and end apart: 5, of which 0 were waited for; matrix products, arithmetic and copies ran while one was open for 11% of the time, Pallas kernels for 0%

commit v1 on v0

--- a/solution.py
+++ b/solution.py
@@ -1,3 +1,4 @@
+import functools
 import math
 
 import jax
@@ -1280,6 +1281,197 @@
     )(cat, note, x, cosine, sine, limit, gate, up, down)
 
 
+def ffn_body(
+    total_tokens, hidden, teacher, valid, notes, gate_w, up_w, down_w,
+    out, grad_hidden, small, gate_sums, up_sums, down_sums,
+    w_gate, w_up, w_down, gate, up, hid, grads_gate, grads_up, inputs_t, cot_t, inputs, cot_b, acc, cot, rate,
+    sums_gate, sums_up, sums_down, load, swap_send, swap_recv, store
+):
+    place = position()
+    x, y, z, c = place
+    other = mesh_place(x, y, z, 1 - c)
+    barrier = pltpu.get_barrier_semaphore()
+    pl.semaphore_signal(barrier, inc=1, device_id=other, device_id_type=MESH_ID)
+    pl.semaphore_wait(barrier, 1)
+    columns = lambda j: lanes_at(j, 768)
+
+    def load_copy(k, source, target, j):
+        return pltpu.make_async_copy(source.at[:, columns(j)], target.at[:, columns(j)], load.at[k, j])
+
+    def loads(j):
+        return [load_copy(k, *pair, j) for k, pair in enumerate(((gate_w, w_gate), (up_w, w_up), (down_w, w_down)))]
+
+    for j in range(4):
+        for copy in loads(j):
+            copy.start()
+
+    def swap(source, target, k):
+        return pltpu.make_async_remote_copy(
+            src_ref=source, dst_ref=target, send_sem=swap_send.at[k], recv_sem=swap_recv.at[k],
+            device_id=other, device_id_type=MESH_ID,
+        )
+
+    own, theirs = pl.ds(0, 256), pl.ds(256, 256)
+    swap_inputs = swap(inputs_t.at[:, own], inputs_t.at[:, theirs], 0)
+    swap_cot = swap(cot_t.at[:, own], cot_t.at[:, theirs], 1)
+
+    def swap_hid(i, core):
+        at = columns(core + 2 * i)
+        return swap(hid.at[own, at], hid.at[theirs, at], 2 + i)
+
+    def swap_grads(ref, j, k):
+        return swap(ref.at[own, columns(j)], ref.at[theirs, columns(j)], k + j)
+
+    def norm(k):
+        rows = rows_at(k, 32)
+        part = hidden[rows, :]
+        scale = lax.rsqrt(jnp.mean(part * part, axis=-1, keepdims=True) + norm_eps)
+        rate[rows, :] = jnp.broadcast_to(scale, (32, 128))
+        inputs[rows, :] = (part * scale * notes[1:2, :]).astype(jnp.bfloat16)
+
+    repeat(8, norm)
+    inputs_t[:, 0:256] = inputs[...].T
+    acc[...] = jnp.zeros_like(acc)
+
+    def forward(j):
+        for copy in loads(j):
+            copy.wait()
+        at = columns(j)
+        gate_part = dot(inputs[...], w_gate[:, at])
+        up_part = dot(inputs[...], w_up[:, at])
+        gate[:, at] = gate_part
+        up[:, at] = up_part
+        hid[0:256, at] = (gate_part * jax.nn.sigmoid(gate_part) * up_part).astype(jnp.bfloat16)
+        acc[...] += dot_t(hid[0:256, at], w_down[:, at])
+
+    repeat(4, forward)
+    swap_inputs.start()
+    for i in range(2):
+        swap_hid(i, 1 - c).start()
+    factor = total_tokens / notes[10:11, :]
+    small[...] = jnp.zeros_like(small)
+
+    def losses(k):
+        rows = rows_at(k, 32)
+        live = valid[rows, 0:1] > 0.0
+        value = jnp.where(live, hidden[rows, :] + acc[rows, :], 0.0)
+        out[rows, :] = value.astype(jnp.bfloat16)
+        diff = jnp.where(live, value - teacher[rows, :].astype(jnp.float32), 0.0)
+        small[2:3, :] += jnp.sum(diff * diff, axis=0, keepdims=True)
+        grad = factor * diff
+        cot[rows, :] = grad
+        cot_b[rows, :] = grad.astype(jnp.bfloat16)
+
+    repeat(8, losses)
+    cot_t[:, 0:256] = cot_b[...].T
+    acc[...] = jnp.zeros_like(acc)
+
+    def backward(j):
+        at = columns(j)
+        grad_hid = dot(cot_b[...], w_down[:, at])
+        gate_part = gate[:, at]
+        sig = jax.nn.sigmoid(gate_part)
+        grads_gate[0:256, at] = (
+            grad_hid * up[:, at] * sig * (1.0 + gate_part * (1.0 - sig))
+        ).astype(jnp.bfloat16)
+        grads_up[0:256, at] = (grad_hid * gate_part * sig).astype(jnp.bfloat16)
+        acc[...] += dot_t(grads_gate[0:256, at], w_gate[:, at]) + dot_t(grads_up[0:256, at], w_up[:, at])
+        swap_grads(grads_gate, j, 4).start()
+        swap_grads(grads_up, j, 8).start()
+        pl.when(j == 0)(swap_cot.start)
+
+    repeat(4, backward)
+
+    def finish_rows(k):
+        rows = rows_at(k, 32)
+        scale = rate[rows, 0:1]
+        normed = hidden[rows, :] * scale
+        grad = acc[rows, :]
+        small[1:2, :] += jnp.sum(grad * normed, axis=0, keepdims=True)
+        grad = grad * notes[1:2, :]
+        inner = grad - normed * jnp.mean(grad * normed, axis=-1, keepdims=True)
+        grad_hidden[rows, :] = cot[rows, :] + scale * inner
+
+    repeat(8, finish_rows)
+    small[2:3, :] = jnp.broadcast_to(jnp.sum(small[2:3, :], axis=-1, keepdims=True), (1, 1152))
+    small[3:4, :] = notes[0:1, :]
+    swap_cot.wait_recv()
+    swap_inputs.wait_recv()
+
+    def stored(k, source, target, i):
+        at = columns(i)
+        return pltpu.make_async_copy(source.at[:, at], target.at[:, at], store.at[k, i])
+
+    def down_grads(i):
+        swap_hid(i, c).wait_recv()
+        sums_down[:, columns(i)] = dot(cot_t[...], hid[:, columns(c + 2 * i)]).astype(jnp.bfloat16)
+        stored(0, sums_down, down_sums, i).start()
+
+    repeat(2, down_grads)
+
+    def wide_grads(j):
+        at = columns(j)
+        swap_grads(grads_gate, j, 4).wait_recv()
+        swap_grads(grads_up, j, 8).wait_recv()
+        for half in range(2):
+            rows = rows_at(c + 2 * half, 288)
+            kept = slice(288 * half, 288 * half + 288)
+            sums_gate[kept, at] = dot(inputs_t[rows, :], grads_gate[:, at]).astype(jnp.bfloat16)
+            sums_up[kept, at] = dot(inputs_t[rows, :], grads_up[:, at]).astype(jnp.bfloat16)
+        stored(1, sums_gate, gate_sums, j).start()
+        stored(2, sums_up, up_sums, j).start()
+
+    repeat(4, wide_grads)
+    swap_inputs.wait_send()
+    swap_cot.wait_send()
+    for i in range(2):
+        swap_hid(i, 1 - c).wait_send()
+        stored(0, sums_down, down_sums, i).wait()
+    for j in range(4):
+        swap_grads(grads_gate, j, 4).wait_send()
+        swap_grads(grads_up, j, 8).wait_send()
+        stored(1, sums_gate, gate_sums, j).wait()
+        stored(2, sums_up, up_sums, j).wait()
+
+
+def ffn_call(total_tokens, hidden, teacher, valid, notes, gate_w, up_w, down_w):
+    vmem, anywhere = pl.BlockSpec(memory_space=pltpu.VMEM), pl.BlockSpec(memory_space=pl.ANY)
+    whole = pltpu.VMEM((1152, 3072), jnp.bfloat16)
+    both = pltpu.VMEM((512, 3072), jnp.bfloat16)
+    return pl.pallas_call(
+        functools.partial(ffn_body, total_tokens),
+        out_shape=[
+            jax.ShapeDtypeStruct((256, 1152), jnp.bfloat16),
+            jax.ShapeDtypeStruct((256, 1152), jnp.float32),
+            jax.ShapeDtypeStruct((8, 1152), jnp.float32),
+            jax.ShapeDtypeStruct((576, 3072), jnp.bfloat16),
+            jax.ShapeDtypeStruct((576, 3072), jnp.bfloat16),
+            jax.ShapeDtypeStruct((1152, 1536), jnp.bfloat16),
+        ],
+        in_specs=[vmem] * 4 + [anywhere] * 3,
+        out_specs=[vmem] * 3 + [anywhere] * 3,
+        scratch_shapes=[whole] * 3
+        + [pltpu.VMEM((256, 3072), jnp.float32)] * 2
+        + [both] * 3
+        + [pltpu.VMEM((1152, 512), jnp.bfloat16)] * 2
+        + [pltpu.VMEM((256, 1152), jnp.bfloat16)] * 2
+        + [pltpu.VMEM((256, 1152), jnp.float32)] * 2
+        + [pltpu.VMEM((256, 128), jnp.float32)]
+        + [pltpu.VMEM((576, 3072), jnp.bfloat16)] * 2
+        + [
+            pltpu.VMEM((1152, 1536), jnp.bfloat16),
+            pltpu.SemaphoreType.DMA((3, 4)),
+            pltpu.SemaphoreType.DMA((12,)),
+            pltpu.SemaphoreType.DMA((12,)),
+            pltpu.SemaphoreType.DMA((3, 4)),
+        ],
+        compiler_params=pltpu.CompilerParams(
+            collective_id=5, has_side_effects=True, vmem_limit_bytes=VMEM_MOST
+        ),
+        name="feed_forward",
+    )(hidden, teacher, valid, notes, gate_w, up_w, down_w)
+
+
 def backward_body(
     grad_hidden, attn_in_t, wcat, keys_values, query, attn, denom, cosine, sine, limit, x, scales, small,
     grad_gate, grad_up, grad_down,
@@ -1515,16 +1707,19 @@
 ):
     slots, part, width = tokens.shape
     rows = slots * part
+    own_columns = gain_attn.shape[0]
+    first_column = lax.axis_index("seq") * own_columns
     total_tokens = slots * lax.axis_size("dp") * part * lax.axis_size("seq")
     positions = lax.axis_index("seq") * part + jnp.arange(part, dtype=jnp.int32)
     cosine, sine = rope_tables(positions, HEAD_DIMENSION)
     cosine_t = jnp.concatenate([cosine.T] * slots, axis=1)
     sine_t = jnp.concatenate([sine.T] * slots, axis=1)
     limit = jnp.minimum(positions[None, :], lengths[:, None] - 1).reshape(1, rows)
+    valid = (positions[None, :] < lengths[:, None]).astype(jnp.float32).reshape(rows, 1)
     note = lax.dynamic_update_slice(
         jnp.zeros((8, width), jnp.float32),
         jnp.stack([gain_attn, gain_ffn]).astype(jnp.float32),
-        (0, lax.axis_index("seq") * gain_attn.shape[0]),
+        (0, first_column),
     )
     note = note.at[2].set(jnp.sum(lengths).astype(jnp.float32))
     x_b = tokens.reshape(rows, width)
@@ -1532,70 +1727,20 @@
         jnp.concatenate([w_query, key_weight, value_weight, w_out], axis=1),
         note, x_b, cosine_t, sine_t, limit, w_gate, w_up, w_down.T,
     )
-    gain_a, gain_f = notes[0:1], notes[1:2]
-    count = notes[10, 0]
-    factor = total_tokens / count
-    r2 = lax.rsqrt(jnp.mean(hidden * hidden, axis=-1, keepdims=True) + norm_eps)
-    n2 = hidden * r2
-    ffn_in = (n2 * gain_f).astype(jnp.bfloat16)
-    gate = dot(ffn_in, gate_w)
-    up = dot(ffn_in, up_w)
-    sig = jax.nn.sigmoid(gate)
-    hid = (gate * sig * up).astype(jnp.bfloat16)
-    valid = (positions[None, :] < lengths[:, None]).reshape(rows, 1)
-    out_f = jnp.where(valid, hidden + dot_t(hid, down_t), 0.0)
-    diff = jnp.where(valid, out_f - teacher.reshape(rows, width).astype(jnp.float32), 0.0)
-    squares = jnp.sum(diff * diff)
-    cot = factor * diff
-    cot_b = cot.astype(jnp.bfloat16)
-    grad_hid = dot(cot_b, down_t)
-    grad_gate_b = (grad_hid * up * sig * (1.0 + gate * (1.0 - sig))).astype(jnp.bfloat16)
-    grad_up_b = (grad_hid * gate * sig).astype(jnp.bfloat16)
-    core = lax.rem(lax.axis_index("dp"), 2)
-
-    def swap(value):
-        return lax.ppermute(value, "dp", [(0, 1), (1, 0), (2, 3), (3, 2)])
-
-    def lane(value, which):
-        parts = value.reshape(rows, 2, 2, value.shape[1] // 4)
-        return lax.dynamic_index_in_dim(parts, which, 2, keepdims=False).reshape(rows, -1)
-
-    def over_cores(value):
-        return jnp.concatenate([value, swap(value)], axis=0)
-
-    def lane_over_cores(value):
-        return jnp.concatenate([lane(value, core), swap(lane(value, 1 - core))], axis=0)
-
-    ffn_lane = lane_over_cores(ffn_in)
-    grad_down_t = t_dot(over_cores(cot_b), lane_over_cores(hid)).astype(jnp.bfloat16)
-    grad_gate_w = t_dot(ffn_lane, over_cores(grad_gate_b)).astype(jnp.bfloat16)
-    grad_up_w = t_dot(ffn_lane, over_cores(grad_up_b)).astype(jnp.bfloat16)
-    grad_ffn_in = dot_t(grad_gate_b, gate_w) + dot_t(grad_up_b, up_w)
-    part_gain_f = jnp.sum(grad_ffn_in * n2, axis=0)
-    gn = grad_ffn_in * gain_f
-    grad_hidden = cot + r2 * (gn - n2 * jnp.mean(gn * n2, axis=-1, keepdims=True))
+    output, grad_hidden, small, gate_sums, up_sums, down_sums = ffn_call(
+        float(total_tokens), hidden, teacher.reshape(rows, width), jnp.broadcast_to(valid, (rows, 128)), notes,
+        gate_w, up_w, down_t,
+    )
     x = x_b.astype(jnp.float32)
     r1 = lax.rsqrt(jnp.mean(x * x, axis=-1, keepdims=True) + norm_eps)
-    small = jnp.concatenate(
-        [
-            jnp.zeros((1, width), jnp.float32),
-            part_gain_f[None, :],
-            jnp.broadcast_to(squares, (1, width)),
-            gain_a,
-            jnp.zeros((4, width), jnp.float32),
-        ],
-        axis=0,
-    )
     own_gate, own_up, own_down_t, own_cat, grad_tokens, totals, _ = backward_call(
         grad_hidden, attn_in_t, cat, keys_values, query, attn, denom, cosine_t, sine_t, limit,
-        x_b, jnp.broadcast_to(r1, (rows, 128)), small, grad_gate_w, grad_up_w, grad_down_t,
-    )
-    own_gains = lax.dynamic_slice(
-        totals, (0, lax.axis_index("seq") * gain_attn.shape[0]), (2, gain_attn.shape[0])
-    )
+        x_b, jnp.broadcast_to(r1, (rows, 128)), small, gate_sums, up_sums, down_sums,
+    )
+    own_gains = lax.dynamic_slice(totals, (0, first_column), (2, own_columns))
     return (
-        out_f.astype(jnp.bfloat16).reshape(tokens.shape),
-        totals[2, 0] / count,
+        output.reshape(tokens.shape),
+        totals[2, 0] / notes[10, 0],
         grad_tokens.reshape(tokens.shape),
         own_cat[:, :144],
         own_cat[:, 144:192],

time: 409 us -> 383 us (0.936); the launches traced: 404 us -> 382 us
  matrix products: 42.8 us -> 0 us
  Pallas kernels: 312 us -> 345 us
  local copies, waits for them, and re-layouts: 36.2 us -> 29.5 us
    dot_general x9 -> x0, matrix products: 42.8 us -> none  [the longest x3 16.6 us: t_dot(): lax.dot_general(a, b, (((0,), (0,)), ((), ())), preferred_element_type=jn...]
    pallas_call x0 -> x1, Pallas kernels: none -> 32.8 us  [ffn_call(): pl.pallas_call(functools.partial(ffn_body, total_tokens), out_shape=[jax....]
    dynamic_slice x2 -> x0, local copies, waits for them, and re-layouts: 5.76 us -> none  [lane(): lax.dynamic_index_in_dim(parts, which, 2, keepdims=False).reshape(rows, -1)]
    reshape x1 -> x0, local copies, waits for them, and re-layouts: 4.24 us -> none  [lane(): parts = value.reshape(rows, 2, 2, value.shape[1] // 4)]
    unnamed x86 -> x49, local copies, waits for them, and re-layouts: 15.7 us -> 19.9 us
  transfers between devices with their start and end apart: 5 -> 0, of which waited for: 0 -> 0; matrix products, arithmetic and copies ran while one was open for 11% -> 0% of each run, Pallas kernels for 0% -> 0%
where the time goes in v1:
time: 383 us; the launch traced here: 382 us
  Pallas kernels  345 us (90%)
  local copies, waits for them, and re-layouts  29.5 us (8%)
  between operations  4 us (1%)
    pallas_call x1, Pallas kernels, backward_call(): pl.pallas_call(backward_body, out_shape=[jax.ShapeDtypeStruct((288, 384),...  163 us
    pallas_call x1, Pallas kernels, forward_call(): pl.pallas_call(forward_body, out_shape=[jax.ShapeDtypeStruct((1152, 3072)...  149 us
    pallas_call x1, Pallas kernels, ffn_call(): pl.pallas_call(functools.partial(ffn_body, total_tokens), out_shape=[jax....  32.8 us
    unnamed x49, local copies, waits for them, and re-layouts  19.9 us

profile of v1, /device:TPU:0, one launch (start us, length us, event | category | flops | bytes accessed | tf_op | source)
XLA Modules:
  0.0 382.1 jit_solution(6164211479925861004)
XLA Ops:
  2.4 1.3 broadcast_add_fusion
  4.8 1.0 copy.24
  5.8 1.0 copy.27
  6.8 0.9 copy.25
  7.7 0.9 copy.26
  8.8 1.1 copy-done
  9.9 0.9 copy-done.7
  10.8 0.9 copy-done.8
  11.8 0.9 copy-done.9
  12.7 148.6 %attention_forward.1 = (bf16[1152,3072]{1,0:T(8,128)(2,1)}, bf16[1152,3072]{1,0:T(8,128)(2,1)}, bf16[1152,3072]{1,0:T(8,128)(2,1)}, bf16[1152,3072]{1,0:T(8,128)...) custom-call(bf16[288,384]{1,0:T(8,128)(2,1)S(1)} %pad_maximum_fusion, ...), custom_call_target="tpu_custom_call" | custom-call | tf_op jit(solution)/shard_map/attention_forward/pallas_call | solution.py:1249
  161.3 1.0 copy-done.1
  162.3 1.0 copy-done.2
  164.1 0.8 copy-done.4
  167.7 32.8 %feed_forward.1 = (bf16[256,1152]{1,0:T(8,128)(2,1)}, f32[256,1152]{1,0:T(8,128)}, f32[8,1152]{1,0:T(8,128)}, bf16[576,3072]{1,0:T(8,128)(2,1)}, bf16[576,3072]{1,0:T(8,128)(2,1)}, /*index=5*/bf16[1152,1536]{1,0:T(8,128)(2,1)}) custom-call(f32[256,1152]{1,0:T(8,128)} %copy-done.2, bf16[256,1152]{1,0:T(8,128)(2,1)} %bitcast.21, ...), custom_call_target="tpu_custom_call" | custom-call | tf_op jit(solution)/shard_map/feed_forward/pallas_call | solution.py:1441
  200.6 1.3 multiply_reduce_fusion
  202.6 163.5 %attention_backward.1 = (f32[288,384]{1,0:T(8,128)}, f32[288,384]{1,0:T(8,128)}, f32[144,768]{1,0:T(8,128)}, f32[288,384]{1,0:T(8,128)}, f32[256,1152]{1,0:T(8,1...) custom-call(f32[256,1152]{1,0:T(8,128)} %get-tuple-element.53.grad_hidden, bf16[1152,256]{1,0:T(8,128)(2,1)} %copy-done.3, ...), custom_call_target="tpu_custom_call" | custom-call | tf_op jit(solution)/shard_map/attention_backward/pallas_call | solution.py:1660
  366.1 1.3 fusion.2
  367.4 0.8 copy.28
  368.3 0.8 copy.31
  369.1 1.1 fusion.3
  371.7 1.4 fusion.4
  373.1 1.2 slice.39
  374.3 1.2 slice.40
  377.7 1.0 copy.40
  (53 shorter events, 11.3 us)
Async XLA Ops:
  4.6 156.7 %copy-start.12 = (s32[2,128]{1,0:T(2,128)}, s32[2,128]{1,0:T(2,128)S(1)}, u32[]{:S(2)}) copy-start(s32[2,128]{1,0:T(2,128)S(1)} %broadcast_minimum_fusion) | copy-start | bytes 3076
  4.8 195.8 %copy-start.5 = (f32[32,256]{1,0:T(8,128)}, f32[32,256]{1,0:T(8,128)S(1)}, u32[]{:S(2)}) copy-start(f32[32,256]{1,0:T(8,128)S(1)} %pad_maximum_fusion.1.cosine) | copy-start | bytes 98308
  4.8 195.8 %copy-start.6 = (f32[32,256]{1,0:T(8,128)}, f32[32,256]{1,0:T(8,128)S(1)}, u32[]{:S(2)}) copy-start(f32[32,256]{1,0:T(8,128)S(1)} %pad_maximum_fusion.2.sine) | copy-start | bytes 98308
  8.8 1.1 copy-start
  9.9 0.9 copy-start.7
  10.8 0.9 copy-start.8
  11.7 0.9 copy-start.9
  161.3 1.0 copy-start.1
  162.3 1.0 copy-start.2
  163.3 0.8 copy-start.3
  164.1 0.8 copy-start.4
  165.0 0.6 copy-start.10
  165.6 0.6 copy-start.11
  366.1 10.8 %copy-start.14 = (bf16[256,1152]{1,0:T(8,128)(2,1)S(1)}, bf16[256,1152]{1,0:T(8,128)(2,1)}, u32[]{:S(2)}) copy-start(bf16[256,1152]{1,0:T(8,128)(2,1)} %get-tuple-element.52) | copy-start | bytes 1769476
  366.1 11.6 %copy-start.13 = (f32[256,1152]{1,0:T(8,128)S(1)}, f32[256,1152]{1,0:T(8,128)}, u32[]{:S(2)}) copy-start(f32[256,1152]{1,0:T(8,128)} %get-tuple-element.65) | copy-start | bytes 3538948
  367.4 12.0 %copy-start.16 = (f32[288,384]{1,0:T(8,128)S(1)}, f32[288,384]{1,0:T(8,128)}, u32[]{:S(2)}) copy-start(f32[288,384]{1,0:T(8,128)} %get-tuple-element.114) | copy-start | bytes 1327108
  368.3 12.0 %copy-start.15 = (f32[144,768]{1,0:T(8,128)S(1)}, f32[144,768]{1,0:T(8,128)}, u32[]{:S(2)}) copy-start(f32[144,768]{1,0:T(8,128)} %get-tuple-element.69) | copy-start | bytes 1327108
  371.0 7.7 %copy-start.17 = (f32[288,384]{1,0:T(8,128)S(1)}, f32[288,384]{1,0:T(8,128)}, u32[]{:S(2)}) copy-start(f32[288,384]{1,0:T(8,128)} %get-tuple-element.113) | copy-start | bytes 1327108

commit v2 on v1

--- a/solution.py
+++ b/solution.py
@@ -1032,36 +1032,36 @@
     (10407, 10413, 10214, 10611, 10614, 10014, 10114, 10515, 10414, 10215, 10314, 10615, 10015, 10115, 10415, 10315,),
 )
 BACKWARD_PLAN = (
-    (10100, 10101,),
+    (),
     (
-        (0, (10300,)),
-        (3, (10000,)),
-        (5, (10102, 10500,)),
-        (8, (10200,)),
-        (9, (10400,)),
+        (0, (10400,)),
+        (3, (10200,)),
+        (4, (10300,)),
+        (5, (10202,)),
+        (6, (20000, 20100, 20200, 20001, 20101, 20002, 20201, 20102, 20202, 10600, 10000, 10001,)),
+        (7, (10201, 20003, 20004, 10301, 20103, 20104,)),
+        (8, (20203, 20204, 20005,)),
+        (9, (10500, 20105, 10401,)),
+        (10, (10303, 20006, 20205,)),
+        (11, (20106, 10302,)),
     ),
-    (10401, 20500, 10103, 10105, 10104, 20000, 10001, 10302, 20501, 20502, 10201, 10501, 10106, 10002, 20300,
-        20100, 20200, 20400, 10202, 10502, 10600, 20504, 20503, 10003, 10304, 10306, 20001, 20101, 20201,
-        20301, 20401, 10107, 10108, 10109, 10110, 20402, 20505, 10301, 10303, 10305, 20002, 20102, 20202,
-        20302, 10203, 10503, 10004, 20506, 20303, 20304, 10204, 10402, 10504, 10005, 10111, 20003, 20103,
-        20203, 20403, 20004, 20204, 20404, 20005, 20205, 10602, 10205, 10604, 20305, 10403, 10505, 10006,
-        20405, 10307, 10308, 10601, 10603, 20006, 20104, 20105, 20106, 10112, 20206, 10206, 10309, 10404,
-        20306, 10506, 10007, 10008, 20007, 20406, 10113, 10009, 10207, 10208, 10209, 10405, 10507, 10508,
-        10509, 20107, 20307, 10310, 10605, 20407, 10010, 20507, 10406, 10210, 10011, 10407, 10408, 10409,
-        20207,),
+    (20400, 20401, 20402, 20206, 10602, 10601, 10402, 20403, 10002, 10203, 20500, 20300, 10603, 10502, 10403,
+        20301, 10100, 10003, 10204, 10305, 10304, 20302, 10604, 10004, 20501, 20303, 10404, 10501, 10503,
+        20007, 10101, 20502, 20504, 20107, 20207, 20503, 20505, 20404, 20405, 10605, 10504, 10205, 10102,
+        10005, 10206, 10405, 10207, 10208, 10209, 10006, 20506, 10306, 20406, 10606, 10406, 10505, 10103,
+        20304, 10307, 10308, 10607, 10608, 10609, 20305, 10506, 10407, 10408, 20306, 10104, 10007, 10008,
+        10009, 10309, 10507, 10508, 10509, 10105, 10409, 20407, 10010, 10310, 10410, 10210, 10106, 20507,
+        10107, 10108, 10109, 20307,),
     (
-        (0, (10311, 10606,)),
-        (2, (10312, 10607, 10608, 10609,)),
-        (3, (10012,)),
-        (4, (10410,)),
-        (7, (10510,)),
+        (3, (10012, 10412,)),
+        (4, (10312, 10011,)),
+        (5, (10311, 10610,)),
     ),
-    (10412, 10411, 10313, 100, 10013, 200, 101, 201, 10114, 10211, 102, 202,),
-    (10610, 103, 203, 10511, 10413, 104, 204,),
-    (10212, 105, 205, 106, 206, 107, 207, 10213, 0, 1, 2, 10611, 3, 10512, 10513, 208, 5, 10612, 108,),
-    (109, 209, 7, 110, 10613, 4, 6, 112, 111, 113, 10314, 210, 10014, 10115, 211, 8, 10, 114, 212,),
-    (9, 213, 10214, 10514, 214, 10414, 10315, 12, 10015, 11, 115, 13, 215, 10215, 10515, 14, 10614, 15, 10415,
-        10615,),
+    (100, 101, 10510, 10411, 10110, 10413, 10013, 0, 10313, 200, 102, 10112, 10211,),
+    (103, 104, 106, 10111, 10212, 105, 10113,),
+    (10014, 10414, 1, 201, 10611, 10314, 107, 2, 202, 10213, 108, 10612, 10511, 3, 203, 205, 109, 10214, 4, 10512,),
+    (204, 5, 10613, 10114, 6, 206, 10614, 110, 112, 10513, 111, 113, 7, 207, 208, 10514, 10015, 10315, 10415, 8,),
+    (209, 114, 10215, 210, 9, 10, 12, 10115, 10615, 115, 211, 212, 213, 11, 13, 10515, 214, 14, 15, 215,),
 )
 
 
@@ -1110,17 +1110,32 @@
     )
 
 
-def three_wide(row):
-    return jnp.concatenate([row] * 3, axis=1)
+def key_limit(length, s):
+    query_pos = s * 128 + lax.broadcasted_iota(jnp.int32, (1, 128), 1)
+    return jnp.concatenate([jnp.minimum(query_pos, length - 1)] * 3, axis=1)
 
 
 def forward_body(
-    cat, note, x, cosine, sine, limit, gate, up, down,
-    gate_w, up_w, down_w, wcat, notes, attn_in_t, hidden, query, keys_values, attn, denom,
+    lengths, query_t, key_t, value_t, out_t, gain_a, gain_f, x, cosine, sine, gate, up, down,
+    gate_w, up_w, down_w, wcat, kept_in_t, kept_query, kept_kv, kept_attn, kept_denom, notes, hidden,
+    tile, cat_t, cat, attn_in_t, query, keys_values, attn, denom,
     attn_in, raw, own_kv, weights, proj, seq_in, dp_in, own_sems, note_a, note_b, note_c, note_d, *sems
 ):
     place = position()
     d, s = mesh_place(*place)
+    row = 0
+    for part in (query_t, key_t, value_t, out_t):
+        cat_t[row: row + part.shape[0], 0:288] = part[...].astype(jnp.float32)
+        row += part.shape[0]
+    cat[...] = cat_t[...].T[0:288, :].astype(jnp.bfloat16)
+    tile[...] = jnp.zeros_like(tile)
+    for k in range(8):
+        def own_gains(k=k):
+            tile[0:1, 144 * k: 144 * k + 144] = gain_a[...].astype(jnp.float32).reshape(1, 144)
+            tile[1:2, 144 * k: 144 * k + 144] = gain_f[...].astype(jnp.float32).reshape(1, 144)
+
+        pl.when(s == k)(own_gains)
+    tile[2:3, :] = jnp.broadcast_to((lengths[0] + lengths[1]).astype(jnp.float32), (1, 1152))
     greet(place, True)
     shards = dict(zip(FFN_NAMES, (gate, up, down)))
     wholes = dict(zip(FFN_NAMES, (gate_w, up_w, down_w)))
@@ -1133,7 +1148,7 @@
         for token in tokens:
             steps[token // 10000][token // 100 % 100][token % 100]()
 
-    tiles = Notes(place, lambda peer: note, note, seq_in, dp_in, (note_a, note_b, note_c, note_d))
+    tiles = Notes(place, lambda peer: tile, tile, seq_in, dp_in, (note_a, note_b, note_c, note_d))
     run(FORWARD_PLAN[0])
     for k in range(1, 8):
         tiles.along_seq(k).start()
@@ -1153,8 +1168,8 @@
     run(FORWARD_PLAN[1])
     tiles.wait_seq()
     tiles.wait_dp()
-    seq_in[s] = note[...]
-    dp_in[d] = note[...]
+    seq_in[s] = tile[...]
+    dp_in[d] = tile[...]
     gains = seq_in[0]
     for k in range(1, 8):
         gains = gains + seq_in[k]
@@ -1192,15 +1207,24 @@
     repeat(6, turn(own_kv, lambda h: rows_at(h, 64, 1152)))
     own_kv[384:768, :] = raw[1536:1920, :].astype(jnp.bfloat16)
     repeat(18, turn(query, lambda h: rows_at(h, 64)))
+    keeps = [
+        pltpu.make_async_copy(source, target, own_sems.at[4 + k])
+        for k, (source, target) in enumerate(
+            ((attn_in_t, kept_in_t), (query, kept_query), (keys_values, kept_kv), (attn, kept_attn), (denom, kept_denom))
+        )
+    ]
+    keeps[0].start()
+    keeps[1].start()
     run(FORWARD_PLAN[3])
     here = lanes_at(s, 128)
     for slot in range(2):
         keys_values[slot, :, here] = own_kv[:, slot * 128: slot * 128 + 128]
     run(FORWARD_PLAN[4])
+    keeps[2].start()
 
     def attend(slot, group):
         lanes = lanes_at(slot, 128)
-        bound = three_wide(limit[:, lanes])
+        bound = key_limit(lengths[slot], s)
         wide = heads_wide(query, group, lanes)
 
         def one_chunk(chunk, carry):
@@ -1225,6 +1249,8 @@
             pl.when(k == at)(lambda tokens=tokens: run(tokens))
 
     repeat(12, unit)
+    keeps[3].start()
+    keeps[4].start()
 
     def out_project(b):
         block = t_dot(attn[...].astype(jnp.bfloat16), weights[:, lanes_at(b, 384)][:, 128:]).T
@@ -1241,26 +1267,26 @@
         tiles.along_seq(k).wait_send()
     for k in range(1, 4):
         tiles.along_dp(k).wait_send()
-    out_copy.wait()
-
-
-def forward_call(cat, note, x, cosine, sine, limit, gate, up, down):
+    for copy in [out_copy] + keeps:
+        copy.wait()
+
+
+def forward_call(lengths, shards_t, gain_a, gain_f, x, cosine, sine, gate, up, down):
     vmem, anywhere = pl.BlockSpec(memory_space=pltpu.VMEM), pl.BlockSpec(memory_space=pl.ANY)
+    kept = [
+        ((1152, 256), jnp.bfloat16), ((1152, 256), jnp.bfloat16), ((2, 768, 1024), jnp.bfloat16),
+        ((1152, 256), jnp.float32), ((6, 8, 256), jnp.float32),
+    ]
     return pl.pallas_call(
         forward_body,
         out_shape=[jax.ShapeDtypeStruct((1152, 3072), jnp.bfloat16)] * 4
+        + [jax.ShapeDtypeStruct(*item) for item in kept]
+        + [jax.ShapeDtypeStruct((16, 1152), jnp.float32), jax.ShapeDtypeStruct((256, 1152), jnp.float32)],
+        in_specs=[pl.BlockSpec(memory_space=pltpu.SMEM)] + [vmem] * 12,
+        out_specs=[anywhere] * 9 + [vmem] * 2,
+        scratch_shapes=[pltpu.VMEM((8, 1152), jnp.float32), pltpu.VMEM((384, 384), jnp.float32), pltpu.VMEM((288, 384), jnp.bfloat16)]
+        + [pltpu.VMEM(*item) for item in kept]
         + [
-            jax.ShapeDtypeStruct((16, 1152), jnp.float32),
-            jax.ShapeDtypeStruct((1152, 256), jnp.bfloat16),
-            jax.ShapeDtypeStruct((256, 1152), jnp.float32),
-            jax.ShapeDtypeStruct((1152, 256), jnp.bfloat16),
-            jax.ShapeDtypeStruct((2, 768, 1024), jnp.bfloat16),
-            jax.ShapeDtypeStruct((1152, 256), jnp.float32),
-            jax.ShapeDtypeStruct((6, 8, 256), jnp.float32),
-        ],
-        in_specs=[vmem] * 9,
-        out_specs=[anywhere] * 4 + [vmem] * 7,
-        scratch_shapes=[
             pltpu.VMEM((256, 1152), jnp.bfloat16),
             pltpu.VMEM((1920, 256), jnp.float32),
             pltpu.VMEM((768, 256), jnp.bfloat16),
@@ -1268,27 +1294,28 @@
             pltpu.VMEM((1152, 256), jnp.float32),
             pltpu.VMEM((8, 8, 1152), jnp.float32),
             pltpu.VMEM((4, 8, 1152), jnp.float32),
-            pltpu.SemaphoreType.DMA((4,)),
+            pltpu.SemaphoreType.DMA((9,)),
         ]
         + NOTE_SEMS
         + spread_sems(CAT_JOBS)
         + spread_sems(FFN_JOBS)
         + spread_sems(KV_JOBS)[:2],
         compiler_params=pltpu.CompilerParams(
-            collective_id=3, has_side_effects=True, vmem_limit_bytes=48 * 1024 * 1024
+            collective_id=3, has_side_effects=True, vmem_limit_bytes=VMEM_MOST
         ),
         name="attention_forward",
-    )(cat, note, x, cosine, sine, limit, gate, up, down)
+    )(lengths, *shards_t, gain_a, gain_f, x, cosine, sine, gate, up, down)
 
 
 def ffn_body(
-    total_tokens, hidden, teacher, valid, notes, gate_w, up_w, down_w,
+    total_tokens, lengths, hidden, teacher, notes, gate_w, up_w, down_w,
     out, grad_hidden, small, gate_sums, up_sums, down_sums,
     w_gate, w_up, w_down, gate, up, hid, grads_gate, grads_up, inputs_t, cot_t, inputs, cot_b, acc, cot, rate,
     sums_gate, sums_up, sums_down, load, swap_send, swap_recv, store
 ):
     place = position()
     x, y, z, c = place
+    _, s = mesh_place(*place)
     other = mesh_place(x, y, z, 1 - c)
     barrier = pltpu.get_barrier_semaphore()
     pl.semaphore_signal(barrier, inc=1, device_id=other, device_id_type=MESH_ID)
@@ -1353,7 +1380,8 @@
 
     def losses(k):
         rows = rows_at(k, 32)
-        live = valid[rows, 0:1] > 0.0
+        first = s * 128 + lax.rem(k, 4) * 32
+        live = first + lax.broadcasted_iota(jnp.int32, (32, 1), 0) < lengths[k // 4]
         value = jnp.where(live, hidden[rows, :] + acc[rows, :], 0.0)
         out[rows, :] = value.astype(jnp.bfloat16)
         diff = jnp.where(live, value - teacher[rows, :].astype(jnp.float32), 0.0)
@@ -1434,7 +1462,7 @@
         stored(2, sums_up, up_sums, j).wait()
 
 
-def ffn_call(total_tokens, hidden, teacher, valid, notes, gate_w, up_w, down_w):
+def ffn_call(total_tokens, lengths, hidden, teacher, notes, gate_w, up_w, down_w):
     vmem, anywhere = pl.BlockSpec(memory_space=pltpu.VMEM), pl.BlockSpec(memory_space=pl.ANY)
     whole = pltpu.VMEM((1152, 3072), jnp.bfloat16)
     both = pltpu.VMEM((512, 3072), jnp.bfloat16)
@@ -1448,7 +1476,7 @@
             jax.ShapeDtypeStruct((576, 3072), jnp.bfloat16),
             jax.ShapeDtypeStruct((1152, 1536), jnp.bfloat16),
         ],
-        in_specs=[vmem] * 4 + [anywhere] * 3,
+        in_specs=[pl.BlockSpec(memory_space=pltpu.SMEM)] + [vmem] * 3 + [anywhere] * 3,
         out_specs=[vmem] * 3 + [anywhere] * 3,
         scratch_shapes=[whole] * 3
         + [pltpu.VMEM((256, 3072), jnp.float32)] * 2
@@ -1469,34 +1497,36 @@
             collective_id=5, has_side_effects=True, vmem_limit_bytes=VMEM_MOST
         ),
         name="feed_forward",
-    )(hidden, teacher, valid, notes, gate_w, up_w, down_w)
+    )(lengths, hidden, teacher, notes, gate_w, up_w, down_w)
 
 
 def backward_body(
-    grad_hidden, attn_in_t, wcat, keys_values, query, attn, denom, cosine, sine, limit, x, scales, small,
+    lengths, grad_hidden, cosine, sine, small, x_in, kept_in_t, wcat, keys_values, kept_query, kept_attn, kept_denom,
     grad_gate, grad_up, grad_down,
-    own_gate, own_up, own_down, own_cat, grad_tokens, totals, grad_cat,
-    weights, whole_kv, part_kv, turned, total, own_kv, left, grad_t, note, seq_in, dp_in, row_sum,
-    load, store, kv_send, kv_recv, kv_arrived, note_a, note_b, note_c, note_d, *scratch
+    own_gate, own_up, own_down, own_query_t, own_key_t, own_value_t, own_out_t, grad_tokens, totals, grad_cat,
+    x, attn_in_t, query, attn, denom, own_cat, weights, whole_kv, part_kv, turned, total, own_kv, left, grad_t, note, seq_in, dp_in, row_sum,
+    load, store, kv_send, kv_recv, *scratch
 ):
     place = position()
     d, s = mesh_place(*place)
     greet(place, True)
     sums = dict(zip(FFN_NAMES, (grad_gate, grad_up, grad_down)))
     owned = dict(zip(FFN_NAMES, (own_gate, own_up, own_down)))
+    kv_arrived, scratch = scratch[: len(FOLD_KV)], scratch[len(FOLD_KV):]
+    note_sems, scratch = scratch[:4], scratch[4:]
     split = len(fold_scratch(FOLD_FFN, False))
     folds = [
         JobFold(place, job, j, sums[job[0]], owned[job[0]], scratch[:split], False) for j, job in enumerate(FOLD_FFN)
     ]
     cat_folds = [JobFold(place, job, j, grad_cat, own_cat, scratch[split:], True) for j, job in enumerate(FOLD_CAT)]
-    tiles = Notes(place, lambda peer: note, row_sum, seq_in, dp_in, (note_a, note_b, note_c, note_d))
+    tiles = Notes(place, lambda peer: note, row_sum, seq_in, dp_in, note_sems)
 
     def kv_fold(j, slot, row, order):
         def out(value):
             own_kv[row: row + 256, slot * 128: slot * 128 + 128] = value
 
         spot = kv_spot(part_kv, slot, row)
-        return Fold(place, order, lambda who: spot(who), kv_arrived.at[j], (kv_send, kv_recv), j, out, kv_amount(part_kv))
+        return Fold(place, order, lambda who: spot(who), kv_arrived[j], (kv_send, kv_recv), j, out, kv_amount(part_kv))
 
     kv_folds = [kv_fold(j, *job) for j, job in enumerate(FOLD_KV)]
     steps = [
@@ -1517,8 +1547,15 @@
         return pltpu.make_async_copy(wcat.at[:, lanes_at(b, 384)], weights.at[:, lanes_at(b, 384)], load.at[b])
 
     repeat(8, lambda b: block_load(b).start())
-    kv_in = pltpu.make_async_copy(keys_values, whole_kv, load.at[8])
-    kv_in.start()
+    kept = [
+        pltpu.make_async_copy(source, target, load.at[8 + k])
+        for k, (source, target) in enumerate(
+            ((keys_values, whole_kv), (kept_query, query), (kept_attn, attn), (kept_denom, denom),
+             (kept_in_t, attn_in_t), (x_in, x))
+        )
+    ]
+    for copy in kept:
+        copy.start()
     grad_t[...] = grad_hidden[...].T.astype(jnp.bfloat16)
     total[...] = jnp.zeros_like(total)
 
@@ -1531,12 +1568,13 @@
 
     repeat(8, out_back)
     run(BACKWARD_PLAN[0])
-    kv_in.wait()
+    for copy in kept:
+        copy.wait()
     scale = HEAD_DIMENSION ** (-0.5)
 
     def attend_back(slot, group):
         lanes = lanes_at(slot, 128)
-        bound = three_wide(limit[:, lanes])
+        bound = key_limit(lengths[slot], s)
         wide = heads_wide(query, group, lanes)
         grads, ratios = [], []
         for i in range(3):
@@ -1617,8 +1655,9 @@
     def finish_rows(k):
         rows = rows_at(k, 32)
         grad = grad_tokens[rows, :]
-        scale_in = scales[rows, 0:1]
-        normed = x[rows, :].astype(jnp.float32) * scale_in
+        normed = x[rows, :].astype(jnp.float32)
+        scale_in = lax.rsqrt(jnp.mean(normed * normed, axis=-1, keepdims=True) + norm_eps)
+        normed = normed * scale_in
         note[0:1, :] += jnp.sum(grad * normed, axis=0, keepdims=True)
         grad = grad * small[3:4, :]
         inner = grad - normed * jnp.mean(grad * normed, axis=-1, keepdims=True)
@@ -1642,6 +1681,11 @@
     tiles.wait_dp()
     dp_in[d] = row_sum[...]
     totals[...] = dp_in[0] + dp_in[1] + dp_in[2] + dp_in[3]
+    turned_cat = own_cat[...].T
+    row = 0
+    for ref in (own_query_t, own_key_t, own_value_t, own_out_t):
+        ref[...] = turned_cat[row: row + ref.shape[0], 0:288]
+        row += ref.shape[0]
     for fold in folds + kv_folds + cat_folds:
         fold.finish()
     for k in range(1, 8):
@@ -1651,26 +1695,26 @@
 
 
 def backward_call(
-    grad_hidden, attn_in_t, wcat, keys_values, query, attn, denom, cosine, sine, limit, x, scales, small,
+    lengths, grad_hidden, cosine, sine, small, x, attn_in_t, wcat, keys_values, query, attn, denom,
     grad_gate, grad_up, grad_down
 ):
     vmem, anywhere = pl.BlockSpec(memory_space=pltpu.VMEM), pl.BlockSpec(memory_space=pl.ANY)
     jobs = len(KV_JOBS)
     most = max(fold_slots(order)[1] for _, _, order in FOLD_KV)
+    outs = ((288, 384), (288, 384), (144, 768), (144, 288), (48, 288), (48, 288), (144, 288), (256, 1152), (8, 1152))
     return pl.pallas_call(
         backward_body,
-        out_shape=[
-            jax.ShapeDtypeStruct((288, 384), jnp.float32),
-            jax.ShapeDtypeStruct((288, 384), jnp.float32),
-            jax.ShapeDtypeStruct((144, 768), jnp.float32),
-            jax.ShapeDtypeStruct((288, 384), jnp.float32),
-            jax.ShapeDtypeStruct((256, 1152), jnp.float32),
-            jax.ShapeDtypeStruct((8, 1152), jnp.float32),
-            jax.ShapeDtypeStruct((1152, 3072), jnp.bfloat16),
-        ],
-        in_specs=[vmem, vmem, anywhere, anywhere] + [vmem] * 9 + [anywhere] * 3,
-        out_specs=[vmem] * 6 + [anywhere],
+        out_shape=[jax.ShapeDtypeStruct(shape, jnp.float32) for shape in outs]
+        + [jax.ShapeDtypeStruct((1152, 3072), jnp.bfloat16)],
+        in_specs=[pl.BlockSpec(memory_space=pltpu.SMEM)] + [vmem] * 4 + [anywhere] * 10,
+        out_specs=[vmem] * len(outs) + [anywhere],
         scratch_shapes=[
+            pltpu.VMEM((256, 1152), jnp.bfloat16),
+            pltpu.VMEM((1152, 256), jnp.bfloat16),
+            pltpu.VMEM((1152, 256), jnp.bfloat16),
+            pltpu.VMEM((1152, 256), jnp.float32),
+            pltpu.VMEM((6, 8, 256), jnp.float32),
+            pltpu.VMEM((384, 384), jnp.float32),
             pltpu.VMEM((1152, 3072), jnp.bfloat16),
             pltpu.VMEM((2, 768, 1024), jnp.bfloat16),
             pltpu.VMEM((2, 768, 1024), jnp.bfloat16),
@@ -1683,12 +1727,12 @@
             pltpu.VMEM((8, 8, 1152), jnp.float32),
             pltpu.VMEM((4, 8, 1152), jnp.float32),
             pltpu.VMEM((8, 1152), jnp.float32),
-            pltpu.SemaphoreType.DMA((9,)),
+            pltpu.SemaphoreType.DMA((14,)),
             pltpu.SemaphoreType.DMA((2,)),
             pltpu.SemaphoreType.DMA((jobs,)),
             pltpu.SemaphoreType.DMA((jobs, most)),
-            pltpu.VMEM((jobs, most, 256, 128), jnp.bfloat16),
         ]
+        + [pltpu.VMEM((fold_slots(order)[1], 256, 128), jnp.bfloat16) for _, _, order in FOLD_KV]
         + NOTE_SEMS
         + fold_scratch(FOLD_FFN, False)
         + fold_scratch(FOLD_CAT, True),
@@ -1697,9 +1741,45 @@
         ),
         name="attention_backward",
     )(
-        grad_hidden, attn_in_t, wcat, keys_values, query, attn, denom, cosine, sine, limit, x, scales, small,
+        lengths, grad_hidden, cosine, sine, small, x, attn_in_t, wcat, keys_values, query, attn, denom,
         grad_gate, grad_up, grad_down,
     )
+
+
+def hand_over_body(count, *refs):
+    sources, (totals, notes) = refs[:count], refs[count: count + 2]
+    targets, (loss, gain_a, gain_f) = refs[count + 2: 2 * count + 2], refs[2 * count + 2: 2 * count + 5]
+    sems = refs[-1]
+    copies = [
+        pltpu.make_async_copy(source, target, sems.at[k]) for k, (source, target) in enumerate(zip(sources, targets))
+    ]
+    for copy in copies:
+        copy.start()
+    loss[...] = totals[2:3, 0:1] / notes[10:11, 0:1]
+    s = lax.axis_index("seq")
+    for k in range(8):
+        def own(k=k):
+            gain_a[...] = totals[0:1, 144 * k: 144 * k + 144]
+            gain_f[...] = totals[1:2, 144 * k: 144 * k + 144]
+
+        pl.when(s == k)(own)
+    for copy in copies:
+        copy.wait()
+
+
+def hand_over(results, totals, notes):
+    vmem, anywhere = pl.BlockSpec(memory_space=pltpu.VMEM), pl.BlockSpec(memory_space=pl.ANY)
+    count = len(results)
+    return pl.pallas_call(
+        functools.partial(hand_over_body, count),
+        out_shape=[jax.ShapeDtypeStruct(r.shape, r.dtype) for r in results]
+        + [jax.ShapeDtypeStruct(shape, jnp.float32) for shape in ((1, 1), (1, 144), (1, 144))],
+        in_specs=[vmem] * (count + 2),
+        out_specs=[anywhere] * count + [vmem] * 3,
+        scratch_shapes=[pltpu.SemaphoreType.DMA((count,))],
+        compiler_params=pltpu.CompilerParams(vmem_limit_bytes=VMEM_MOST),
+        name="hand_over",
+    )(*results, totals, notes)
 
 
 def per_device_fast(
@@ -1707,50 +1787,41 @@
 ):
     slots, part, width = tokens.shape
     rows = slots * part
-    own_columns = gain_attn.shape[0]
-    first_column = lax.axis_index("seq") * own_columns
     total_tokens = slots * lax.axis_size("dp") * part * lax.axis_size("seq")
     positions = lax.axis_index("seq") * part + jnp.arange(part, dtype=jnp.int32)
     cosine, sine = rope_tables(positions, HEAD_DIMENSION)
     cosine_t = jnp.concatenate([cosine.T] * slots, axis=1)
     sine_t = jnp.concatenate([sine.T] * slots, axis=1)
-    limit = jnp.minimum(positions[None, :], lengths[:, None] - 1).reshape(1, rows)
-    valid = (positions[None, :] < lengths[:, None]).astype(jnp.float32).reshape(rows, 1)
-    note = lax.dynamic_update_slice(
-        jnp.zeros((8, width), jnp.float32),
-        jnp.stack([gain_attn, gain_ffn]).astype(jnp.float32),
-        (0, first_column),
-    )
-    note = note.at[2].set(jnp.sum(lengths).astype(jnp.float32))
     x_b = tokens.reshape(rows, width)
-    gate_w, up_w, down_t, cat, notes, attn_in_t, hidden, query, keys_values, attn, denom = forward_call(
-        jnp.concatenate([w_query, key_weight, value_weight, w_out], axis=1),
-        note, x_b, cosine_t, sine_t, limit, w_gate, w_up, w_down.T,
+    gate_w, up_w, down_t, cat, attn_in_t, query, keys_values, attn, denom, notes, hidden = forward_call(
+        lengths, (w_query.T, key_weight.T, value_weight.T, w_out.T),
+        gain_attn, gain_ffn, x_b, cosine_t, sine_t,
+        w_gate, w_up, w_down.T,
     )
     output, grad_hidden, small, gate_sums, up_sums, down_sums = ffn_call(
-        float(total_tokens), hidden, teacher.reshape(rows, width), jnp.broadcast_to(valid, (rows, 128)), notes,
-        gate_w, up_w, down_t,
-    )
-    x = x_b.astype(jnp.float32)
-    r1 = lax.rsqrt(jnp.mean(x * x, axis=-1, keepdims=True) + norm_eps)
-    own_gate, own_up, own_down_t, own_cat, grad_tokens, totals, _ = backward_call(
-        grad_hidden, attn_in_t, cat, keys_values, query, attn, denom, cosine_t, sine_t, limit,
-        x_b, jnp.broadcast_to(r1, (rows, 128)), small, gate_sums, up_sums, down_sums,
-    )
-    own_gains = lax.dynamic_slice(totals, (0, first_column), (2, own_columns))
+        float(total_tokens), lengths, hidden, teacher.reshape(rows, width), notes, gate_w, up_w, down_t
+    )
+    *results, totals, _ = backward_call(
+        lengths, grad_hidden, cosine_t, sine_t, small, x_b, attn_in_t, cat, keys_values, query, attn, denom,
+        gate_sums, up_sums, down_sums,
+    )
+    (
+        output, own_gate, own_up, own_down_t, own_query_t, own_key_t, own_value_t, own_out_t, grad_tokens,
+        loss, own_gain_a, own_gain_f,
+    ) = hand_over([output] + results, totals, notes)
     return (
         output.reshape(tokens.shape),
-        totals[2, 0] / notes[10, 0],
+        loss.reshape(()),
         grad_tokens.reshape(tokens.shape),
-        own_cat[:, :144],
-        own_cat[:, 144:192],
-        own_cat[:, 192:240],
-        own_cat[:, 240:],
+        own_query_t.T,
+        own_key_t.T,
+        own_value_t.T,
+        own_out_t.T,
         own_gate,
         own_up,
         own_down_t.T,
-        own_gains[0],
-        own_gains[1],
+        own_gain_a.reshape(-1),
+        own_gain_f.reshape(-1),
     )
 
 

time: 383 us -> 349 us (0.911)
  local copies, waits for them, and re-layouts: 29.5 us -> 0 us
    unnamed x49 -> x0, local copies, waits for them, and re-layouts: 19.9 us -> none
    slice x5 -> x0, local copies, waits for them, and re-layouts: 6.25 us -> none  [the longest x1 1.42 us: per_device_fast(): own_gains[1]]
    pallas_call x1 -> x2, Pallas kernels: 163 us -> 166 us  [the longest x1 161 us: backward_call(): pl.pallas_call(backward_body, out_shape=[jax.ShapeDtypeStruct(shape, jnp....]
where the time goes in v2:
time: 349 us
  Pallas kernels  348 us (100%)
    pallas_call x1, Pallas kernels, backward_call(): pl.pallas_call(backward_body, out_shape=[jax.ShapeDtypeStruct(shape, jnp....  161 us
    pallas_call x1, Pallas kernels, forward_call(): pl.pallas_call(forward_body, out_shape=[jax.ShapeDtypeStruct((1152, 3072)...  149 us
    pallas_call x1, Pallas kernels, ffn_call(): pl.pallas_call(functools.partial(ffn_body, total_tokens), out_shape=[jax....  32.5 us

profile of v2, /device:TPU:0, one launch (start us, length us, event | category | flops | bytes accessed | tf_op | source)
XLA Modules:
  0.0 349.2 jit_solution(2116413455235661539)
XLA Ops:
  0.7 0.1 multiply_sine_fusion
  0.8 0.6 pad_maximum_fusion
  1.5 149.5 %attention_forward.1 = (bf16[1152,3072]{1,0:T(8,128)(2,1)}, bf16[1152,3072]{1,0:T(8,128)(2,1)}, bf16[1152,3072]{1,0:T(8,128)(2,1)}, bf16[1152,3072]{1,0:T(8,128)...) custom-call(s32[2]{0:T(128)} %lengths.5, ...), custom_call_target="tpu_custom_call" | custom-call | tf_op jit(solution)/shard_map/attention_forward/pallas_call | solution.py:1280
  150.9 32.5 %feed_forward.1 = (bf16[256,1152]{1,0:T(8,128)(2,1)}, f32[256,1152]{1,0:T(8,128)}, f32[8,1152]{1,0:T(8,128)}, bf16[576,3072]{1,0:T(8,128)(2,1)}, bf16[576,3072]{1,0:T(8,128)(2,1)}, /*index=5*/bf16[1152,1536]{1,0:T(8,128)(2,1)}) custom-call(s32[2]{0:T(128)} %lengths.5, f32[256,1152]{1,0:T(8,128)} %get-tuple-element.50.hidden, bf16[256,1152]{1,0:T(8,128)(2,1)} %bitcast.19, ...), custom_call_target="tpu_custom_call" | custom-call | tf_op jit(solution)/shard_map/feed_forward/pallas_call | solution.py:1469
  183.4 161.0 %attention_backward.1 = (f32[288,384]{1,0:T(8,128)}, f32[288,384]{1,0:T(8,128)}, f32[144,768]{1,0:T(8,128)}, f32[144,288]{1,0:T(8,128)}, f32[48,288]{1,0:T(8,128...) custom-call(s32[2]{0:T(128)} %lengths.5, ...), custom_call_target="tpu_custom_call" | custom-call | tf_op jit(solution)/shard_map/attention_backward/pallas_call | solution.py:1705
  344.5 4.6 %hand_over.1 = (bf16[256,1152]{1,0:T(8,128)(2,1)}, f32[288,384]{1,0:T(8,128)}, f32[288,384]{1,0:T(8,128)}, f32[144,768]{1,0:T(8,128)}, f32[144,288]{1,0:T(8,128)...) custom-call(bf16[256,1152]{1,0:T(8,128)(2,1)} %get-tuple-element.55., ...), custom_call_target="tpu_custom_call" | custom-call | tf_op jit(solution)/shard_map/hand_over/pallas_call | solution.py:1773
  (2 shorter events, 0.0 us)

commit v3 on v2

--- a/solution.py
+++ b/solution.py
@@ -785,9 +785,9 @@
 CAT_JOBS = (("cat", 0, 96, "xzy"), ("cat", 96, 96, "yzx"), ("cat", 192, 96, "zxy"))
 FFN_JOBS = (
     ("gate", 0, 144, "xzy"), ("up", 0, 96, "yzx"), ("down", 0, 384, "zxy"),
-    ("gate", 144, 144, "xzy"), ("up", 96, 96, "yzx"), ("down", 384, 384, "zxy"), ("up", 192, 96, "zxy"),
+    ("gate", 144, 144, "xzy"), ("up", 96, 96, "yzx"), ("down", 384, 384, "zxy"), ("up", 192, 96, "zyx"),
 )
-KV_JOBS = tuple((slot, 256 * third, "xz" if (slot, third) == (1, 2) else "zx") for slot in (0, 1) for third in (0, 1, 2))
+KV_JOBS = tuple((slot, 256 * third, "zx") for slot in (0, 1) for third in (0, 1, 2))
 FOLD_FFN = tuple(job[:3] + (job[3][::-1],) for job in FFN_JOBS)
 FOLD_CAT = tuple(job[:3] + (job[3][::-1],) for job in CAT_JOBS)
 FOLD_KV = tuple((slot, row, order[::-1]) for slot, row, order in KV_JOBS)
@@ -1006,62 +1006,68 @@
 
 
 FORWARD_PLAN = (
-    (0, 100, 200,),
-    (108, 1, 2, 101, 102, 8, 201, 204, 208, 4, 3, 202, 9, 104, 103, 205, 10, 109, 110, 209, 5, 105, 206, 203,
-        11, 210, 6, 212, 106, 112, 207, 7, 213, 107,),
-    (10500, 113, 211, 114, 10000, 10600, 214, 115, 14, 111, 10100, 10200, 10300, 10400, 12, 215, 15, 13,),
+    (200, 0, 100,),
+    (2, 1, 201, 204, 101, 102, 4, 202, 3, 8, 205, 208, 108, 104, 103, 203, 5, 206, 9, 109, 209, 105, 10, 110,
+        6, 212, 207, 106, 210, 7, 112, 10500, 12, 11,),
+    (111, 107, 213, 10200, 113, 211, 10600, 214, 13, 10000, 10300, 10400, 114, 215, 14, 115, 15,),
     (20000, 20100, 20200, 20300, 20400, 20500,),
-    (10002, 10001, 20001, 20101, 20002, 20004, 10504, 20201, 20104, 10204, 20301, 20204, 10102, 20401, 10501,
-        20304, 10101, 10008, 10201, 20502, 10604, 20501, 20404, 10108, 10302, 10301, 10601, 10402, 10401,
-        20102, 10508, 10004, 10208, 20202, 10308, 10408, 20302, 10608, 10104, 20402, 20005, 10202, 10009,
-        20105, 10502, 20205, 10209, 10304, 10003, 10404, 10010, 10602, 20503, 20504, 20305, 20405, 10509,
-        10103, 10309, 10505, 10205, 20003, 10609, 10303, 10109, 10110, 10310, 20103, 20006, 10605, 20203,
-        10403, 20505, 20106, 10005, 20303, 10210, 20206, 10512, 10409, 10410, 10510, 10212, 20306, 10613,
-        20406, 10506, 10203, 10105, 10503, 10612, 10206, 10305, 10610, 10012, 10405, 20403, 10603, 10606,
-        20107, 10011, 10213, 20007, 10006, 10312, 20506, 20207, 10513, 10111, 10112, 20307, 10311, 10507,
-        20507, 10511, 10411, 20407,),
+    (10100, 20001, 20004, 20101, 20201, 20104, 20301, 20204, 10201, 10002, 10001, 20401, 20304, 10204, 20501,
+        10501, 20404, 20002, 10208, 20504, 10008, 10504, 20102, 10508, 10301, 10302, 20202, 10402, 10601,
+        20005, 20302, 10308, 10401, 10408, 20205, 20402, 10604, 10608, 10102, 20502, 10101, 20305, 10108,
+        10202, 20405, 10004, 20505, 10502, 10209, 10009, 10010, 20105, 10205, 20003, 10003, 10304, 10509,
+        20103, 10602, 20006, 10605, 10505, 20203, 10404, 10212, 10104, 10309, 10310, 20106, 20303, 20403,
+        10303, 20206, 10512, 20306, 20503, 10005, 10403, 10210, 20406, 10103, 10409, 10510, 10110, 10609,
+        20506, 10410, 10305, 10109, 10213, 10513, 10203, 10012, 10405, 10503, 10011, 10105, 10612, 10206,
+        20007, 10506, 10606, 10013, 20107, 10603, 10613, 10312, 10610, 20207, 10311, 10006, 20307, 10211,
+        10313, 20407, 10511, 20507,),
     (
-        (1, (10211, 10306, 10412,)),
-        (2, (10207, 10106, 10013, 10607,)),
-        (3, (10406,)),
-        (5, (10007,)),
-        (8, (10113,)),
-        (9, (10107, 10514,)),
-        (11, (10307, 10313,)),
+        (1, (10412,)),
+        (3, (10411,)),
+        (4, (10007, 10207,)),
+        (5, (10306, 10413, 10112, 10406, 10214,)),
+        (6, (10507,)),
+        (7, (10111, 10514,)),
+        (8, (10607, 10106,)),
+        (9, (10307,)),
+        (10, (10407,)),
     ),
-    (10407, 10413, 10214, 10611, 10614, 10014, 10114, 10515, 10414, 10215, 10314, 10615, 10015, 10115, 10415, 10315,),
+    (10113, 10611, 10107, 10014, 10614, 10415, 10515, 10215, 10314, 10615, 10015, 10114, 10414, 10315, 10115,),
 )
 BACKWARD_PLAN = (
-    (),
     (
-        (0, (10400,)),
-        (3, (10200,)),
-        (4, (10300,)),
-        (5, (10202,)),
-        (6, (20000, 20100, 20200, 20001, 20101, 20002, 20201, 20102, 20202, 10600, 10000, 10001,)),
-        (7, (10201, 20003, 20004, 10301, 20103, 20104,)),
-        (8, (20203, 20204, 20005,)),
-        (9, (10500, 20105, 10401,)),
-        (10, (10303, 20006, 20205,)),
-        (11, (20106, 10302,)),
+        (10100, 10101, 10102, 10104, 10103, 10300,),
+        (10000, 10105, 10002, 10301,),
     ),
-    (20400, 20401, 20402, 20206, 10602, 10601, 10402, 20403, 10002, 10203, 20500, 20300, 10603, 10502, 10403,
-        20301, 10100, 10003, 10204, 10305, 10304, 20302, 10604, 10004, 20501, 20303, 10404, 10501, 10503,
-        20007, 10101, 20502, 20504, 20107, 20207, 20503, 20505, 20404, 20405, 10605, 10504, 10205, 10102,
-        10005, 10206, 10405, 10207, 10208, 10209, 10006, 20506, 10306, 20406, 10606, 10406, 10505, 10103,
-        20304, 10307, 10308, 10607, 10608, 10609, 20305, 10506, 10407, 10408, 20306, 10104, 10007, 10008,
-        10009, 10309, 10507, 10508, 10509, 10105, 10409, 20407, 10010, 10310, 10410, 10210, 10106, 20507,
-        10107, 10108, 10109, 20307,),
     (
-        (3, (10012, 10412,)),
-        (4, (10312, 10011,)),
-        (5, (10311, 10610,)),
+        (1, (10001, 10500,)),
+        (2, (10302, 10106, 10200,)),
+        (3, (10501,)),
+        (5, (10107, 10108,)),
+        (6, (20000, 20100, 20001, 20002, 20101, 20200, 20201, 20102, 20003, 20103, 20202, 10303, 10003, 10109,
+            10401, 20004,)),
+        (7, (20203, 10502, 20104, 10004, 10400,)),
+        (8, (10304, 10110,)),
+        (9, (20005,)),
+        (10, (20204, 20006, 10201,)),
+        (11, (20105, 20106, 10503, 10402,)),
     ),
-    (100, 101, 10510, 10411, 10110, 10413, 10013, 0, 10313, 200, 102, 10112, 10211,),
-    (103, 104, 106, 10111, 10212, 105, 10113,),
-    (10014, 10414, 1, 201, 10611, 10314, 107, 2, 202, 10213, 108, 10612, 10511, 3, 203, 205, 109, 10214, 4, 10512,),
-    (204, 5, 10613, 10114, 6, 206, 10614, 110, 112, 10513, 111, 113, 7, 207, 208, 10514, 10015, 10315, 10415, 8,),
-    (209, 114, 10215, 210, 9, 10, 12, 10115, 10615, 115, 211, 212, 213, 11, 13, 10515, 214, 14, 15, 215,),
+    (20500, 20300, 20400, 20401, 20301, 20302, 20402, 20303, 20403, 10305, 10202, 20205, 10504, 20007, 10111,
+        20206, 10306, 10601, 10600, 20107, 20501, 20502, 20503, 10403, 10112, 10005, 10505, 10203, 10307,
+        10308, 10602, 20207, 10204, 10404, 10506, 10007, 10603, 10006, 10008, 10309, 10205, 10405, 10507,
+        10508, 10509, 20404, 20504, 10009, 10604, 10010, 20304, 10605, 10310, 20405, 10207, 20305, 20306,
+        10206, 10208, 10209, 10407, 20406, 20505, 20506, 10311, 10012, 10510, 10312, 10011, 10210, 10113,
+        20307, 10406, 10408, 10409, 10410, 20407, 10607, 10606, 10608, 10609, 20507,),
+    (
+        (3, (10411,)),
+        (4, (10610,)),
+        (7, (10412,)),
+    ),
+    (10511, 10211, 10114, 10313, 0, 1, 2, 3, 100, 102, 200, 201,),
+    (202, 203, 10013, 101, 4, 204,),
+    (206, 103, 5, 105, 205, 104, 106, 6, 7, 207, 10512, 10212, 10014, 10413, 107, 8, 208, 10611, 10115,),
+    (209, 108, 9, 10314, 109, 10, 12, 10612, 110, 112, 210, 11, 13, 111, 113, 211, 212, 10414,),
+    (10513, 10514, 14, 10315, 114, 10015, 10213, 10214, 10613, 213, 214, 15, 10614, 115, 215, 10515, 10415,
+        10215, 10615,),
 )
 
 
@@ -1556,6 +1562,7 @@
     ]
     for copy in kept:
         copy.start()
+    run(BACKWARD_PLAN[0][0])
     grad_t[...] = grad_hidden[...].T.astype(jnp.bfloat16)
     total[...] = jnp.zeros_like(total)
 
@@ -1567,7 +1574,7 @@
         total[...] += dot(weights[:, lanes_at(b, 384)][:, 128:], out_rows(b))
 
     repeat(8, out_back)
-    run(BACKWARD_PLAN[0])
+    run(BACKWARD_PLAN[0][1])
     for copy in kept:
         copy.wait()
     scale = HEAD_DIMENSION ** (-0.5)
@@ -1749,12 +1756,11 @@
 def hand_over_body(count, *refs):
     sources, (totals, notes) = refs[:count], refs[count: count + 2]
     targets, (loss, gain_a, gain_f) = refs[count + 2: 2 * count + 2], refs[2 * count + 2: 2 * count + 5]
-    sems = refs[-1]
-    copies = [
-        pltpu.make_async_copy(source, target, sems.at[k]) for k, (source, target) in enumerate(zip(sources, targets))
-    ]
-    for copy in copies:
-        copy.start()
+    held, (into, out) = refs[2 * count + 5: 3 * count + 5], refs[-2:]
+    reads = [pltpu.make_async_copy(source, there, into.at[k]) for k, (source, there) in enumerate(zip(sources, held))]
+    copies = [pltpu.make_async_copy(there, target, out.at[k]) for k, (there, target) in enumerate(zip(held, targets))]
+    for read in reads:
+        read.start()
     loss[...] = totals[2:3, 0:1] / notes[10:11, 0:1]
     s = lax.axis_index("seq")
     for k in range(8):
@@ -1763,6 +1769,9 @@
             gain_f[...] = totals[1:2, 144 * k: 144 * k + 144]
 
         pl.when(s == k)(own)
+    for read, copy in zip(reads, copies):
+        read.wait()
+        copy.start()
     for copy in copies:
         copy.wait()
 
@@ -1774,9 +1783,10 @@
         functools.partial(hand_over_body, count),
         out_shape=[jax.ShapeDtypeStruct(r.shape, r.dtype) for r in results]
         + [jax.ShapeDtypeStruct(shape, jnp.float32) for shape in ((1, 1), (1, 144), (1, 144))],
-        in_specs=[vmem] * (count + 2),
+        in_specs=[anywhere] * count + [vmem] * 2,
         out_specs=[anywhere] * count + [vmem] * 3,
-        scratch_shapes=[pltpu.SemaphoreType.DMA((count,))],
+        scratch_shapes=[pltpu.VMEM(r.shape, r.dtype) for r in results]
+        + [pltpu.SemaphoreType.DMA((count,)), pltpu.SemaphoreType.DMA((count,))],
         compiler_params=pltpu.CompilerParams(vmem_limit_bytes=VMEM_MOST),
         name="hand_over",
     )(*results, totals, notes)

time: 349 us -> 340 us (0.974)
  Pallas kernels: 348 us -> 338 us
    pallas_call x1, Pallas kernels: 161 us -> 155 us  [backward_call(): pl.pallas_call(backward_body, out_shape=[jax.ShapeDtypeStruct(shape, jnp....]
    pallas_call x1, Pallas kernels: 149 us -> 145 us  [forward_call(): pl.pallas_call(forward_body, out_shape=[jax.ShapeDtypeStruct((1152, 3072)...]
where the time goes in v3:
time: 340 us
  Pallas kernels  338 us (99%)
    pallas_call x1, Pallas kernels, backward_call(): pl.pallas_call(backward_body, out_shape=[jax.ShapeDtypeStruct(shape, jnp....  155 us
    pallas_call x1, Pallas kernels, forward_call(): pl.pallas_call(forward_body, out_shape=[jax.ShapeDtypeStruct((1152, 3072)...  145 us
    pallas_call x1, Pallas kernels, ffn_call(): pl.pallas_call(functools.partial(ffn_body, total_tokens), out_shape=[jax....  32.3 us

profile of v3, /device:TPU:0, one launch (start us, length us, event | category | flops | bytes accessed | tf_op | source)
XLA Modules:
  0.0 339.6 jit_solution(406328556543908356)
XLA Ops:
  0.7 0.1 multiply_sine_fusion
  0.8 0.6 pad_maximum_fusion
  1.5 145.3 %attention_forward.1 = (bf16[1152,3072]{1,0:T(8,128)(2,1)}, bf16[1152,3072]{1,0:T(8,128)(2,1)}, bf16[1152,3072]{1,0:T(8,128)(2,1)}, bf16[1152,3072]{1,0:T(8,128)...) custom-call(s32[2]{0:T(128)} %lengths.5, ...), custom_call_target="tpu_custom_call" | custom-call | tf_op jit(solution)/shard_map/attention_forward/pallas_call | solution.py:1286
  146.8 32.3 %feed_forward.1 = (bf16[256,1152]{1,0:T(8,128)(2,1)}, f32[256,1152]{1,0:T(8,128)}, f32[8,1152]{1,0:T(8,128)}, bf16[576,3072]{1,0:T(8,128)(2,1)}, bf16[576,3072]{1,0:T(8,128)(2,1)}, /*index=5*/bf16[1152,1536]{1,0:T(8,128)(2,1)}) custom-call(s32[2]{0:T(128)} %lengths.5, f32[256,1152]{1,0:T(8,128)} %get-tuple-element.50.hidden, bf16[256,1152]{1,0:T(8,128)(2,1)} %bitcast.19, ...), custom_call_target="tpu_custom_call" | custom-call | tf_op jit(solution)/shard_map/feed_forward/pallas_call | solution.py:1475
  179.1 155.5 %attention_backward.1 = (f32[288,384]{1,0:T(8,128)}, f32[288,384]{1,0:T(8,128)}, f32[144,768]{1,0:T(8,128)}, f32[144,288]{1,0:T(8,128)}, f32[48,288]{1,0:T(8,128...) custom-call(s32[2]{0:T(128)} %lengths.5, ...), custom_call_target="tpu_custom_call" | custom-call | tf_op jit(solution)/shard_map/attention_backward/pallas_call | solution.py:1712
  334.6 4.8 %hand_over.1 = (bf16[256,1152]{1,0:T(8,128)(2,1)}, f32[288,384]{1,0:T(8,128)}, f32[288,384]{1,0:T(8,128)}, f32[144,768]{1,0:T(8,128)}, f32[144,288]{1,0:T(8,128)...) custom-call(bf16[256,1152]{1,0:T(8,128)(2,1)} %get-tuple-element.55., ...), custom_call_target="tpu_custom_call" | custom-call | tf_op jit(solution)/shard_map/hand_over/pallas_call | solution.py:1782
  (2 shorter events, 0.0 us)

commit v4 on v3

--- a/solution.py
+++ b/solution.py
@@ -1035,39 +1035,39 @@
 )
 BACKWARD_PLAN = (
     (
-        (10100, 10101, 10102, 10104, 10103, 10300,),
-        (10000, 10105, 10002, 10301,),
+        (10100, 10102, 10101, 10103, 10104, 10106, 10105, 10400, 10200,),
+        (10401, 10107, 10108, 10109, 10110, 10201,),
     ),
     (
-        (1, (10001, 10500,)),
-        (2, (10302, 10106, 10200,)),
-        (3, (10501,)),
-        (5, (10107, 10108,)),
-        (6, (20000, 20100, 20001, 20002, 20101, 20200, 20201, 20102, 20003, 20103, 20202, 10303, 10003, 10109,
-            10401, 20004,)),
-        (7, (20203, 10502, 20104, 10004, 10400,)),
-        (8, (10304, 10110,)),
-        (9, (20005,)),
-        (10, (20204, 20006, 10201,)),
-        (11, (20105, 20106, 10503, 10402,)),
+        (0, (10000, 10402, 10300,)),
+        (1, (10301,)),
+        (2, (10202,)),
+        (3, (10204,)),
+        (4, (10403,)),
+        (5, (10112,)),
+        (6, (20000, 20100, 20200, 20001, 20101, 20201, 20002, 20102, 20202, 20003, 20103, 20203, 10111, 10203,
+            10500, 10302, 10002, 20004,)),
+        (7, (10113, 20104,)),
+        (8, (10404, 20204,)),
+        (9, (20005, 20105, 10501, 10303,)),
+        (10, (10601, 20006, 20205,)),
+        (11, (20106,)),
     ),
-    (20500, 20300, 20400, 20401, 20301, 20302, 20402, 20303, 20403, 10305, 10202, 20205, 10504, 20007, 10111,
-        20206, 10306, 10601, 10600, 20107, 20501, 20502, 20503, 10403, 10112, 10005, 10505, 10203, 10307,
-        10308, 10602, 20207, 10204, 10404, 10506, 10007, 10603, 10006, 10008, 10309, 10205, 10405, 10507,
-        10508, 10509, 20404, 20504, 10009, 10604, 10010, 20304, 10605, 10310, 20405, 10207, 20305, 20306,
-        10206, 10208, 10209, 10407, 20406, 20505, 20506, 10311, 10012, 10510, 10312, 10011, 10210, 10113,
-        20307, 10406, 10408, 10409, 10410, 20407, 10607, 10606, 10608, 10609, 20507,),
+    (20500, 20501, 20502, 20503, 20300, 20400, 20401, 20402, 20403, 20301, 20206, 10600, 10602, 10502, 10405,
+        10304, 10306, 10004, 10205, 10406, 10407, 10408, 20302, 20303, 10305, 10410, 20007, 10001, 10003,
+        10005, 10503, 10006, 10409, 20107, 10604, 20504, 20505, 20207, 20506, 10206, 10207, 10208, 10209,
+        10210, 10603, 10504, 10007, 10008, 10307, 10308, 10010, 10505, 20304, 10009, 10310, 20404, 10605,
+        10412, 10114, 10506, 10606, 20305, 20306, 20405, 10411, 10507, 10508, 10509, 10309, 20406, 10510,
+        10012, 20507, 10607, 10608, 10609, 10011, 10610, 10312, 10211, 20407, 10311, 10413, 20307,),
     (
-        (3, (10411,)),
-        (4, (10610,)),
-        (7, (10412,)),
+        (0, (10013,)),
+        (5, (10313, 10115,)),
     ),
-    (10511, 10211, 10114, 10313, 0, 1, 2, 3, 100, 102, 200, 201,),
-    (202, 203, 10013, 101, 4, 204,),
-    (206, 103, 5, 105, 205, 104, 106, 6, 7, 207, 10512, 10212, 10014, 10413, 107, 8, 208, 10611, 10115,),
-    (209, 108, 9, 10314, 109, 10, 12, 10612, 110, 112, 210, 11, 13, 111, 113, 211, 212, 10414,),
-    (10513, 10514, 14, 10315, 114, 10015, 10213, 10214, 10613, 213, 214, 15, 10614, 115, 215, 10515, 10415,
-        10215, 10615,),
+    (10511, 10414, 10212, 10014, 10611, 10213, 10214, 10314, 200, 201, 202,),
+    (203, 205, 204, 206, 0, 1,),
+    (10415, 2, 207, 3, 208, 10512, 4, 5, 10612, 10015, 6, 10613, 10614, 10513, 209, 10514, 7,),
+    (10315, 10215, 100, 102, 210, 104, 106, 8, 101, 103, 211, 105, 9, 107, 10, 11, 212,),
+    (10615, 12, 10515, 13, 213, 214, 108, 109, 110, 14, 112, 215, 111, 113, 114, 15, 115,),
 )
 
 

time: 340 us -> 336 us (0.988)
  Pallas kernels: 338 us -> 334 us
    pallas_call x1, Pallas kernels: 155 us -> 152 us  [backward_call(): pl.pallas_call(backward_body, out_shape=[jax.ShapeDtypeStruct(shape, jnp....]
where the time goes in v4:
time: 336 us
  Pallas kernels  334 us (99%)
    pallas_call x1, Pallas kernels, backward_call(): pl.pallas_call(backward_body, out_shape=[jax.ShapeDtypeStruct(shape, jnp....  152 us
    pallas_call x1, Pallas kernels, forward_call(): pl.pallas_call(forward_body, out_shape=[jax.ShapeDtypeStruct((1152, 3072)...  145 us
    pallas_call x1, Pallas kernels, ffn_call(): pl.pallas_call(functools.partial(ffn_body, total_tokens), out_shape=[jax....  32.3 us

profile of v4, /device:TPU:0, one launch (start us, length us, event | category | flops | bytes accessed | tf_op | source)
XLA Modules:
  0.0 335.7 jit_solution(7981105412828274334)
XLA Ops:
  0.7 0.1 multiply_sine_fusion
  0.8 0.6 pad_maximum_fusion
  1.5 145.3 %attention_forward.1 = (bf16[1152,3072]{1,0:T(8,128)(2,1)}, bf16[1152,3072]{1,0:T(8,128)(2,1)}, bf16[1152,3072]{1,0:T(8,128)(2,1)}, bf16[1152,3072]{1,0:T(8,128)...) custom-call(s32[2]{0:T(128)} %lengths.5, ...), custom_call_target="tpu_custom_call" | custom-call | tf_op jit(solution)/shard_map/attention_forward/pallas_call | solution.py:1286
  146.8 32.3 %feed_forward.1 = (bf16[256,1152]{1,0:T(8,128)(2,1)}, f32[256,1152]{1,0:T(8,128)}, f32[8,1152]{1,0:T(8,128)}, bf16[576,3072]{1,0:T(8,128)(2,1)}, bf16[576,3072]{1,0:T(8,128)(2,1)}, /*index=5*/bf16[1152,1536]{1,0:T(8,128)(2,1)}) custom-call(s32[2]{0:T(128)} %lengths.5, f32[256,1152]{1,0:T(8,128)} %get-tuple-element.50.hidden, bf16[256,1152]{1,0:T(8,128)(2,1)} %bitcast.19, ...), custom_call_target="tpu_custom_call" | custom-call | tf_op jit(solution)/shard_map/feed_forward/pallas_call | solution.py:1475
  179.1 151.7 %attention_backward.1 = (f32[288,384]{1,0:T(8,128)}, f32[288,384]{1,0:T(8,128)}, f32[144,768]{1,0:T(8,128)}, f32[144,288]{1,0:T(8,128)}, f32[48,288]{1,0:T(8,128...) custom-call(s32[2]{0:T(128)} %lengths.5, ...), custom_call_target="tpu_custom_call" | custom-call | tf_op jit(solution)/shard_map/attention_backward/pallas_call | solution.py:1712
  330.8 4.8 %hand_over.1 = (bf16[256,1152]{1,0:T(8,128)(2,1)}, f32[288,384]{1,0:T(8,128)}, f32[288,384]{1,0:T(8,128)}, f32[144,768]{1,0:T(8,128)}, f32[144,288]{1,0:T(8,128)...) custom-call(bf16[256,1152]{1,0:T(8,128)(2,1)} %get-tuple-element.55., ...), custom_call_target="tpu_custom_call" | custom-call | tf_op jit(solution)/shard_map/hand_over/pallas_call | solution.py:1782
  (2 shorter events, 0.0 us)

commit v5 on v4

--- a/solution.py
+++ b/solution.py
@@ -1007,31 +1007,33 @@
 
 FORWARD_PLAN = (
     (200, 0, 100,),
-    (2, 1, 201, 204, 101, 102, 4, 202, 3, 8, 205, 208, 108, 104, 103, 203, 5, 206, 9, 109, 209, 105, 10, 110,
-        6, 212, 207, 106, 210, 7, 112, 10500, 12, 11,),
-    (111, 107, 213, 10200, 113, 211, 10600, 214, 13, 10000, 10300, 10400, 114, 215, 14, 115, 15,),
-    (20000, 20100, 20200, 20300, 20400, 20500,),
-    (10100, 20001, 20004, 20101, 20201, 20104, 20301, 20204, 10201, 10002, 10001, 20401, 20304, 10204, 20501,
-        10501, 20404, 20002, 10208, 20504, 10008, 10504, 20102, 10508, 10301, 10302, 20202, 10402, 10601,
-        20005, 20302, 10308, 10401, 10408, 20205, 20402, 10604, 10608, 10102, 20502, 10101, 20305, 10108,
-        10202, 20405, 10004, 20505, 10502, 10209, 10009, 10010, 20105, 10205, 20003, 10003, 10304, 10509,
-        20103, 10602, 20006, 10605, 10505, 20203, 10404, 10212, 10104, 10309, 10310, 20106, 20303, 20403,
-        10303, 20206, 10512, 20306, 20503, 10005, 10403, 10210, 20406, 10103, 10409, 10510, 10110, 10609,
-        20506, 10410, 10305, 10109, 10213, 10513, 10203, 10012, 10405, 10503, 10011, 10105, 10612, 10206,
-        20007, 10506, 10606, 10013, 20107, 10603, 10613, 10312, 10610, 20207, 10311, 10006, 20307, 10211,
-        10313, 20407, 10511, 20507,),
+    (1, 2, 201, 8, 101, 102, 204, 3, 208, 4, 108, 9, 109, 104, 202, 103, 10, 205, 110, 209, 5, 105, 206, 212,
+        203, 6, 11, 210, 12, 111, 112, 106, 7, 207,),
+    (10500, 107, 211, 10200, 10300, 10400, 10000, 10100, 10600, 213, 113, 13, 114, 214, 215, 115, 14, 15,),
+    (20200, 20300, 20500, 20400, 20000, 20100,),
+    (20201, 20204, 20301, 20304, 10001, 20001, 20004, 20401, 10504, 10204, 20504, 20002, 20404, 10501, 20501,
+        10201, 20101, 20104, 10102, 10101, 10108, 10008, 10002, 10301, 20202, 20005, 20302, 10302, 10508,
+        10208, 10408, 10402, 10401, 20102, 10308, 10601, 20205, 20402, 20502, 10604, 20305, 10608, 10004,
+        20405, 20505, 10104, 10009, 20105, 10509, 10202, 10502, 10304, 10209, 20003, 10404, 20006, 20203,
+        10309, 10602, 20303, 20206, 10205, 10010, 10212, 20103, 10505, 10109, 10605, 10003, 20106, 20306,
+        10512, 20403, 20503, 10110, 20406, 10310, 20506, 10103, 10005, 10303, 10609, 10409, 10105, 10410,
+        10305, 10012, 10210, 10403, 10405, 10510, 10011, 20007, 10612, 10311, 10312, 10206, 20207, 10606,
+        10506, 10513, 20307, 10503, 10112, 10203, 10213, 20107, 10006, 20407, 20507,),
     (
-        (1, (10412,)),
-        (3, (10411,)),
-        (4, (10007, 10207,)),
-        (5, (10306, 10413, 10112, 10406, 10214,)),
-        (6, (10507,)),
-        (7, (10111, 10514,)),
-        (8, (10607, 10106,)),
-        (9, (10307,)),
-        (10, (10407,)),
+        (0, (10412,)),
+        (1, (10111, 10106,)),
+        (2, (10610,)),
+        (3, (10306, 10511,)),
+        (4, (10211,)),
+        (5, (10406, 10603,)),
+        (6, (10013,)),
+        (7, (10613, 10411, 10514,)),
+        (8, (10007,)),
+        (9, (10107, 10313, 10214,)),
+        (10, (10207, 10507,)),
+        (11, (10307, 10607,)),
     ),
-    (10113, 10611, 10107, 10014, 10614, 10415, 10515, 10215, 10314, 10615, 10015, 10114, 10414, 10315, 10115,),
+    (10407, 10113, 10611, 10014, 10413, 10614, 10314, 10114, 10414, 10515, 10215, 10015, 10115, 10615, 10415, 10315,),
 )
 BACKWARD_PLAN = (
     (
@@ -1367,14 +1369,16 @@
     acc[...] = jnp.zeros_like(acc)
 
     def forward(j):
-        for copy in loads(j):
-            copy.wait()
         at = columns(j)
+        from_gate, from_up, from_down = loads(j)
+        from_gate.wait()
         gate_part = dot(inputs[...], w_gate[:, at])
+        from_up.wait()
         up_part = dot(inputs[...], w_up[:, at])
         gate[:, at] = gate_part
         up[:, at] = up_part
         hid[0:256, at] = (gate_part * jax.nn.sigmoid(gate_part) * up_part).astype(jnp.bfloat16)
+        from_down.wait()
         acc[...] += dot_t(hid[0:256, at], w_down[:, at])
 
     repeat(4, forward)

time: 336 us -> 336 us (level)
  no operation moved by 1% of the time
where the time goes in v5:
time: 336 us
  Pallas kernels  334 us (99%)
    pallas_call x1, Pallas kernels, backward_call(): pl.pallas_call(backward_body, out_shape=[jax.ShapeDtypeStruct(shape, jnp....  152 us
    pallas_call x1, Pallas kernels, forward_call(): pl.pallas_call(forward_body, out_shape=[jax.ShapeDtypeStruct((1152, 3072)...  143 us
    pallas_call x1, Pallas kernels, ffn_call(): pl.pallas_call(functools.partial(ffn_body, total_tokens), out_shape=[jax....  34.1 us

profile of v5, /device:TPU:0, one launch (start us, length us, event | category | flops | bytes accessed | tf_op | source)
XLA Modules:
  0.0 336.1 jit_solution(17287603106332680304)
XLA Ops:
  0.7 0.1 multiply_sine_fusion
  0.8 0.6 pad_maximum_fusion
  1.5 143.4 %attention_forward.1 = (bf16[1152,3072]{1,0:T(8,128)(2,1)}, bf16[1152,3072]{1,0:T(8,128)(2,1)}, bf16[1152,3072]{1,0:T(8,128)(2,1)}, bf16[1152,3072]{1,0:T(8,128)...) custom-call(s32[2]{0:T(128)} %lengths.5, ...), custom_call_target="tpu_custom_call" | custom-call | tf_op jit(solution)/shard_map/attention_forward/pallas_call | solution.py:1288
  144.9 34.1 %feed_forward.1 = (bf16[256,1152]{1,0:T(8,128)(2,1)}, f32[256,1152]{1,0:T(8,128)}, f32[8,1152]{1,0:T(8,128)}, bf16[576,3072]{1,0:T(8,128)(2,1)}, bf16[576,3072]{1,0:T(8,128)(2,1)}, /*index=5*/bf16[1152,1536]{1,0:T(8,128)(2,1)}) custom-call(s32[2]{0:T(128)} %lengths.5, f32[256,1152]{1,0:T(8,128)} %get-tuple-element.50.hidden, bf16[256,1152]{1,0:T(8,128)(2,1)} %bitcast.19, ...), custom_call_target="tpu_custom_call" | custom-call | tf_op jit(solution)/shard_map/feed_forward/pallas_call | solution.py:1479
  179.0 152.1 %attention_backward.1 = (f32[288,384]{1,0:T(8,128)}, f32[288,384]{1,0:T(8,128)}, f32[144,768]{1,0:T(8,128)}, f32[144,288]{1,0:T(8,128)}, f32[48,288]{1,0:T(8,128...) custom-call(s32[2]{0:T(128)} %lengths.5, ...), custom_call_target="tpu_custom_call" | custom-call | tf_op jit(solution)/shard_map/attention_backward/pallas_call | solution.py:1716
  331.1 4.8 %hand_over.1 = (bf16[256,1152]{1,0:T(8,128)(2,1)}, f32[288,384]{1,0:T(8,128)}, f32[288,384]{1,0:T(8,128)}, f32[144,768]{1,0:T(8,128)}, f32[144,288]{1,0:T(8,128)...) custom-call(bf16[256,1152]{1,0:T(8,128)(2,1)} %get-tuple-element.55., ...), custom_call_target="tpu_custom_call" | custom-call | tf_op jit(solution)/shard_map/hand_over/pallas_call | solution.py:1786
  (2 shorter events, 0.0 us)

commit v6 on v5

--- a/solution.py
+++ b/solution.py
@@ -1763,8 +1763,9 @@
     held, (into, out) = refs[2 * count + 5: 3 * count + 5], refs[-2:]
     reads = [pltpu.make_async_copy(source, there, into.at[k]) for k, (source, there) in enumerate(zip(sources, held))]
     copies = [pltpu.make_async_copy(there, target, out.at[k]) for k, (there, target) in enumerate(zip(held, targets))]
-    for read in reads:
-        read.start()
+    largest_first = sorted(range(count), key=lambda k: -math.prod(held[k].shape))
+    for k in largest_first:
+        reads[k].start()
     loss[...] = totals[2:3, 0:1] / notes[10:11, 0:1]
     s = lax.axis_index("seq")
     for k in range(8):
@@ -1773,9 +1774,9 @@
             gain_f[...] = totals[1:2, 144 * k: 144 * k + 144]
 
         pl.when(s == k)(own)
-    for read, copy in zip(reads, copies):
-        read.wait()
-        copy.start()
+    for k in largest_first:
+        reads[k].wait()
+        copies[k].start()
     for copy in copies:
         copy.wait()
 

time: 336 us -> 336 us (level)
  no operation moved by 1% of the time
where the time goes in v6:
time: 336 us
  Pallas kernels  334 us (99%)
    pallas_call x1, Pallas kernels, backward_call(): pl.pallas_call(backward_body, out_shape=[jax.ShapeDtypeStruct(shape, jnp....  152 us
    pallas_call x1, Pallas kernels, forward_call(): pl.pallas_call(forward_body, out_shape=[jax.ShapeDtypeStruct((1152, 3072)...  143 us
    pallas_call x1, Pallas kernels, ffn_call(): pl.pallas_call(functools.partial(ffn_body, total_tokens), out_shape=[jax....  34.1 us

profile of v6, /device:TPU:0, one launch (start us, length us, event | category | flops | bytes accessed | tf_op | source)
XLA Modules:
  0.0 336.0 jit_solution(17345139679982080117)
XLA Ops:
  0.7 0.1 multiply_sine_fusion
  0.8 0.6 pad_maximum_fusion
  1.5 143.4 %attention_forward.1 = (bf16[1152,3072]{1,0:T(8,128)(2,1)}, bf16[1152,3072]{1,0:T(8,128)(2,1)}, bf16[1152,3072]{1,0:T(8,128)(2,1)}, bf16[1152,3072]{1,0:T(8,128)...) custom-call(s32[2]{0:T(128)} %lengths.5, ...), custom_call_target="tpu_custom_call" | custom-call | tf_op jit(solution)/shard_map/attention_forward/pallas_call | solution.py:1288
  144.9 34.1 %feed_forward.1 = (bf16[256,1152]{1,0:T(8,128)(2,1)}, f32[256,1152]{1,0:T(8,128)}, f32[8,1152]{1,0:T(8,128)}, bf16[576,3072]{1,0:T(8,128)(2,1)}, bf16[576,3072]{1,0:T(8,128)(2,1)}, /*index=5*/bf16[1152,1536]{1,0:T(8,128)(2,1)}) custom-call(s32[2]{0:T(128)} %lengths.5, f32[256,1152]{1,0:T(8,128)} %get-tuple-element.50.hidden, bf16[256,1152]{1,0:T(8,128)(2,1)} %bitcast.19, ...), custom_call_target="tpu_custom_call" | custom-call | tf_op jit(solution)/shard_map/feed_forward/pallas_call | solution.py:1479
  179.0 152.1 %attention_backward.1 = (f32[288,384]{1,0:T(8,128)}, f32[288,384]{1,0:T(8,128)}, f32[144,768]{1,0:T(8,128)}, f32[144,288]{1,0:T(8,128)}, f32[48,288]{1,0:T(8,128...) custom-call(s32[2]{0:T(128)} %lengths.5, ...), custom_call_target="tpu_custom_call" | custom-call | tf_op jit(solution)/shard_map/attention_backward/pallas_call | solution.py:1716
  331.1 4.7 %hand_over.1 = (bf16[256,1152]{1,0:T(8,128)(2,1)}, f32[288,384]{1,0:T(8,128)}, f32[288,384]{1,0:T(8,128)}, f32[144,768]{1,0:T(8,128)}, f32[144,288]{1,0:T(8,128)...) custom-call(bf16[256,1152]{1,0:T(8,128)(2,1)} %get-tuple-element.55., ...), custom_call_target="tpu_custom_call" | custom-call | tf_op jit(solution)/shard_map/hand_over/pallas_call | solution.py:1787
  (2 shorter events, 0.0 us)
